TPU v7x, 32 devices: a whole 2x2x4 slice. The times are simulated.
32 devices in a mesh: rows: 8 (over y, x, core), cols: 4 (over z).
Axes of the slice: x: 2, y: 2, z: 4, core: 2. Of those that a mesh axis runs over, the one named last changes fastest.
Arguments:
- raw_panel: float32 [256, 32768], P('cols', 'rows')
- raw_trail: float32 [1024, 32768], P('cols', 'rows')
- panel_shift: int32 [256], P('cols'), may hold values from 0 to 255, as said below
- trail_shift: int32 [1024], P('cols'), may hold values from 0 to 255, as said below
Outputs:
- r_factor: float32 [256, 256], replicated
- coupling: float32 [256, 1024], P(None, 'cols')
- q_panel: float32 [256, 32768], P('cols', 'rows')
- trail_out: float32 [1024, 32768], P('cols', 'rows')
Inputs may be any that keep to these rules, and one draw needn't show every extreme that they name: `panel_shift`: among the 64 panel and 256 trailing PSFs held by one index of cols, at most 40 have the same value of shift // 32, and exactly 40 share some value. `trail_shift`: as for panel_shift, over the same PSFs of one index of cols.
All inputs are finite; a program needn't handle non-finite values.
Results may differ from a plain program's by a relative error of at most 0.0003.
Values sent between devices are 32-bit elements; how exact they have to be, the bound alone decides.
A program may use at most 64 MiB of HBM per device.

v0:
```python
import functools
import math

import jax
import jax.numpy as jnp
from jax import lax
from jax.experimental import pallas as pl
from jax.experimental.pallas import tpu as pltpu
from jax.sharding import PartitionSpec as P

BW = 128
MESH = pl.DeviceIdType.MESH


def roll_rows(n, blocks, first, count, shift_ref, ring, moved):
    total = n * blocks

    def one(k, carry):
        shift = shift_ref[first + k]
        ring[k, pl.ds(total, blocks), :] = ring[k, pl.ds(0, blocks), :]
        for j in range(n):
            start = lax.rem(j * blocks - shift + total, total)
            moved[j, k] = ring[k, pl.ds(start, blocks), :]
        return carry

    lax.fori_loop(0, count, one, 0)


def exchange_kernel(
    n,
    depth,
    pieces,
    chunks,
    panel_shift,
    trail_shift,
    panel,
    trail,
    full,
    back,
    moved_b,
    ring_p,
    moved_p,
    moved_a,
    p1_send,
    p1_recv,
    t1_send,
    t1_recv,
    p2_send,
    p2_recv,
    t2_send,
    t2_recv,
    z_send,
    z_recv,
    local_sem,
    *rings,
):
    me = lax.axis_index("rows")
    z = lax.axis_index("cols")
    kp, blocks = panel.shape[1], panel.shape[2]
    kt = trail.shape[1]
    part = kt // chunks
    width = n // pieces * kp
    mine = pl.ds(pl.multiple_of(me * blocks, blocks), blocks)
    place = pl.ds(me * kp, kp)

    barrier = pltpu.get_barrier_semaphore()
    for d in range(1, n):
        pl.semaphore_signal(
            barrier, inc=1, device_id={"rows": lax.rem(me + d, n)}, device_id_type=MESH
        )

    @pl.when(z > 0)
    def _():
        pl.semaphore_signal(barrier, inc=1, device_id={"cols": z - 1}, device_id_type=MESH)

    @pl.when(z < depth - 1)
    def _():
        pl.semaphore_signal(barrier, inc=1, device_id={"cols": z + 1}, device_id_type=MESH)

    sides = jnp.where(z > 0, 1, 0) + jnp.where(z < depth - 1, 1, 0)
    pl.semaphore_wait(barrier, n - 1 + sides)

    def row_copy(src, dst, send, recv, to):
        return pltpu.make_async_remote_copy(
            src_ref=src,
            dst_ref=dst,
            send_sem=send,
            recv_sem=recv,
            device_id={"rows": to},
            device_id_type=MESH,
        )

    far = [lax.rem(me + d, n) for d in range(1, n)]
    p1 = [
        row_copy(panel.at[to], ring_p.at[:, mine], p1_send.at[i], p1_recv.at[i], to)
        for i, to in enumerate(far)
    ]
    own_p1 = pltpu.make_async_copy(panel.at[me], ring_p.at[:, mine], local_sem.at[0])
    t1, own_t1 = [], []
    for c in range(chunks):
        span = pl.ds(c * part, part)
        t1.append(
            [
                row_copy(
                    trail.at[to, span],
                    rings[c].at[:, mine],
                    t1_send.at[c, i],
                    t1_recv.at[c, i],
                    to,
                )
                for i, to in enumerate(far)
            ]
        )
        own_t1.append(
            pltpu.make_async_copy(
                trail.at[me, span], rings[c].at[:, mine], local_sem.at[2 + c]
            )
        )
    p2 = [
        row_copy(moved_p.at[to], full.at[z, place], p2_send.at[i], p2_recv.at[i], to)
        for i, to in enumerate(far)
    ]
    t2 = [
        row_copy(moved_a.at[to], back.at[me], t2_send.at[i], t2_recv.at[i], to)
        for i, to in enumerate(far)
    ]
    own_t2 = pltpu.make_async_copy(moved_a.at[me], back.at[me], local_sem.at[2 + chunks])
    own_p2 = pltpu.make_async_copy(moved_p.at[me], full.at[z, place], local_sem.at[1])

    def line(side, d, q):
        step = 1 if side == 0 else -1
        origin = z - step * (d - 1)
        rows = pl.ds(q * width, width)
        return pltpu.make_async_remote_copy(
            src_ref=full.at[origin, rows],
            dst_ref=full.at[origin, rows],
            send_sem=z_send.at[side, d - 1, q],
            recv_sem=z_recv.at[side, d - 1, q],
            device_id={"cols": z + step},
            device_id_type=MESH,
        )

    def sends(side, d):
        if side == 0:
            return (z + 1 < depth) & (z - (d - 1) >= 0)
        return (z >= 1) & (z + (d - 1) < depth)

    def receives(side, d):
        return z - d >= 0 if side == 0 else z + d < depth

    def arrived(side, d, q):
        step = 1 if side == 0 else -1
        origin = z - step * d
        rows = pl.ds(q * width, width)
        return pltpu.make_async_remote_copy(
            src_ref=full.at[origin, rows],
            dst_ref=full.at[origin, rows],
            send_sem=z_send.at[side, d - 1, q],
            recv_sem=z_recv.at[side, d - 1, q],
            device_id={"cols": z - step},
            device_id_type=MESH,
        )

    def forward(d):
        for q in range(pieces):
            for side in (0, 1):

                @pl.when(receives(side, d))
                def _():
                    arrived(side, d, q).wait_recv()

                if d + 1 < depth:

                    @pl.when(sends(side, d + 1))
                    def _():
                        line(side, d + 1, q).start()

    own_p1.start()
    for copy in p1:
        copy.start()
    own_p1.wait()
    for copy in p1:
        copy.wait_recv()
    roll_rows(n, blocks, 0, kp, panel_shift, ring_p, moved_p)
    own_p2.start()
    for copy in p2:
        copy.start()
    for c in range(chunks):
        own_t1[c].start()
        for copy in t1[c]:
            copy.start()
    own_p2.wait()
    for copy in p2:
        copy.wait_recv()
    for q in range(pieces):
        for side in (0, 1):

            @pl.when(sends(side, 1))
            def _():
                line(side, 1, q).start()

    forward(1)
    own_t1[0].wait()
    for copy in t1[0]:
        copy.wait_recv()
    roll_rows(n, blocks, 0, part, trail_shift, rings[0], moved_a)
    own_t2.start()
    for copy in t2:
        copy.start()
    if depth > 2:
        forward(2)
    own_t1[1].wait()
    for copy in t1[1]:
        copy.wait_recv()
    roll_rows(n, blocks, part, part, trail_shift, rings[1], moved_b)
    for d in range(3, depth):
        forward(d)
    own_t2.wait()
    for copy in t2:
        copy.wait_recv()
    for copy in p1 + p2 + t1[0] + t1[1] + t2:
        copy.wait_send()
    for d in range(1, depth):
        for q in range(pieces):
            for side in (0, 1):

                @pl.when(sends(side, d))
                def _():
                    line(side, d, q).wait_send()


def exchange(panel, trail, panel_shift, trail_shift, n, depth):
    _, kp, blocks, _ = panel.shape
    kt = trail.shape[1]
    pieces = 4 if n % 4 == 0 else 1
    chunks = 2
    half = jax.ShapeDtypeStruct((n, kt // 2, blocks, BW), jnp.float32)
    f32 = jnp.float32
    smem = pl.BlockSpec(memory_space=pltpu.SMEM)
    vmem = pl.BlockSpec(memory_space=pltpu.VMEM)
    hbm = pl.BlockSpec(memory_space=pl.ANY)
    dma = pltpu.SemaphoreType.DMA
    return pl.pallas_call(
        functools.partial(exchange_kernel, n, depth, pieces, chunks),
        out_shape=(
            jax.ShapeDtypeStruct((depth, n * kp, blocks, BW), f32),
            half,
            half,
        ),
        in_specs=[smem, smem, hbm, hbm],
        out_specs=(vmem,) * 3,
        scratch_shapes=[
            pltpu.VMEM((kp, (n + 1) * blocks, BW), f32),
            pltpu.VMEM((n, kp, blocks, BW), f32),
            pltpu.VMEM(half.shape, f32),
            dma((n - 1,)),
            dma((n - 1,)),
            dma((chunks, n - 1)),
            dma((chunks, n - 1)),
            dma((n - 1,)),
            dma((n - 1,)),
            dma((n - 1,)),
            dma((n - 1,)),
            dma((2, max(depth - 1, 1), pieces)),
            dma((2, max(depth - 1, 1), pieces)),
            dma((3 + chunks,)),
        ]
        + [pltpu.VMEM((kt // chunks, (n + 1) * blocks, BW), f32)] * chunks,
        compiler_params=pltpu.CompilerParams(collective_id=3, has_side_effects=True),
        cost_estimate=pl.CostEstimate(
            flops=0, bytes_accessed=40 * trail.size * 4, transcendentals=0
        ),
    )(panel_shift, trail_shift, panel, trail)


def grouped(raw, shifts, n, my_row, unit):
    rows, pixels = raw.shape
    padded = -(-rows // (n * unit)) * n * unit
    if padded != rows:
        raw = jnp.pad(raw, ((0, padded - rows), (0, 0)))
        shifts = jnp.pad(shifts, (0, padded - rows))
    count = padded // n
    mine = lax.dynamic_slice_in_dim(shifts, my_row * count, count, 0)
    return raw.reshape(n, count, pixels // BW, BW), mine


def inner_rows(left, right, precision):
    return lax.dot_general(
        left,
        right,
        (((1,), (1,)), ((), ())),
        precision=precision,
        preferred_element_type=jnp.float32,
    )


def sum_kernel(n, part_ref, out_ref, landed, send_one, recv_one, send_two, recv_two):
    me = lax.axis_index("rows")
    barrier = pltpu.get_barrier_semaphore()
    for d in range(1, n):
        pl.semaphore_signal(
            barrier, inc=1, device_id={"rows": lax.rem(me + d, n)}, device_id_type=MESH
        )
    pl.semaphore_wait(barrier, n - 1)
    scatter = []
    for d in range(1, n):
        to = lax.rem(me + d, n)
        copy = pltpu.make_async_remote_copy(
            src_ref=part_ref.at[to],
            dst_ref=landed.at[d - 1],
            send_sem=send_one.at[d - 1],
            recv_sem=recv_one.at[d - 1],
            device_id={"rows": to},
            device_id_type=MESH,
        )
        copy.start()
        scatter.append(copy)
    total = part_ref[me]
    for d in range(1, n):
        scatter[d - 1].wait_recv()
        total = total + landed[d - 1]
    out_ref[me] = total
    spread = []
    for d in range(1, n):
        to = lax.rem(me + d, n)
        copy = pltpu.make_async_remote_copy(
            src_ref=out_ref.at[me],
            dst_ref=out_ref.at[me],
            send_sem=send_two.at[d - 1],
            recv_sem=recv_two.at[d - 1],
            device_id={"rows": to},
            device_id_type=MESH,
        )
        copy.start()
        spread.append(copy)
    for copy in scatter:
        copy.wait_send()
    for copy in spread:
        copy.wait_recv()
    for copy in spread:
        copy.wait_send()


def sum_rows(part, n, ident):
    rows, columns = part.shape
    cut = (n, rows // n, columns)
    out = pl.pallas_call(
        functools.partial(sum_kernel, n),
        out_shape=jax.ShapeDtypeStruct(cut, jnp.float32),
        in_specs=[pl.BlockSpec(memory_space=pltpu.VMEM)],
        out_specs=pl.BlockSpec(memory_space=pltpu.VMEM),
        scratch_shapes=[pltpu.VMEM((n - 1,) + cut[1:], jnp.float32)]
        + [pltpu.SemaphoreType.DMA((n - 1,))] * 4,
        compiler_params=pltpu.CompilerParams(collective_id=ident, has_side_effects=True),
        cost_estimate=pl.CostEstimate(
            flops=0, bytes_accessed=16 * part.size * 4, transcendentals=0
        ),
    )(part.reshape(cut))
    return out.reshape(rows, columns)


def factor_kernel(size, tile, scale, gram_ref, upper_ref, inv_ref, aug, pair):
    grow = lax.broadcasted_iota(jnp.int32, (size, size), 0)
    gcol = lax.broadcasted_iota(jnp.int32, (size, size), 1)
    aug[:, 0:size] = gram_ref[...]
    aug[:, size : 2 * size] = jnp.where(grow == gcol, 1.0, 0.0)
    row = lax.broadcasted_iota(jnp.int32, (tile, 2 * tile), 0)
    col = lax.broadcasted_iota(jnp.int32, (tile, 2 * tile), 1)
    for lo in range(0, size, tile):
        hi = lo + tile
        pair[...] = jnp.where(col == row + tile, 1.0, 0.0)
        pair[:, 0:tile] = aug[lo:hi, lo:hi]
        w = pair[...]
        pivots = jnp.zeros((tile, 1), jnp.float32)
        for j in range(tile):
            base = j // 8 * 8
            live = w[base:, :]
            lead = w[j : j + 1, :]
            pivot = lead[:, j : j + 1]
            pivots = jnp.where(row[:, 0:1] == j, pivot, pivots)
            if j + 1 == tile:
                break
            mult = jnp.where(row[base:, 0:1] > j, live[:, j : j + 1], 0.0)
            live = live - mult * (lead / pivot)
            w = live if base == 0 else jnp.concatenate([w[:base], live], axis=0)
        pair[...] = w * (1.0 / jnp.sqrt(pivots))
        inverse = pair[:, tile : 2 * tile]
        lead_rows = lax.dot_general(
            inverse,
            aug[lo:hi, :],
            (((1,), (0,)), ((), ())),
            precision=lax.Precision.HIGHEST,
            preferred_element_type=jnp.float32,
        )
        keep = gcol[lo:hi] >= grow[lo:hi]
        upper = jnp.where(keep, lead_rows[:, 0:size], 0.0)
        upper_ref[lo:hi, :] = upper * scale
        inv_ref[lo:hi, :] = lead_rows[:, size : 2 * size]
        if hi < size:
            aug[...] = aug[...] - lax.dot_general(
                upper,
                lead_rows,
                (((0,), (0,)), ((), ())),
                precision=lax.Precision.HIGHEST,
                preferred_element_type=jnp.float32,
            )


def factor(gram, scale):
    size = gram.shape[0]
    tile = min(64, size)
    square = jax.ShapeDtypeStruct((size, size), jnp.float32)
    return pl.pallas_call(
        functools.partial(factor_kernel, size, tile, scale),
        out_shape=(square, square),
        in_specs=[pl.BlockSpec(memory_space=pltpu.VMEM)],
        out_specs=(pl.BlockSpec(memory_space=pltpu.VMEM),) * 2,
        scratch_shapes=[
            pltpu.VMEM((size, 2 * size), jnp.float32),
            pltpu.VMEM((tile, 2 * tile), jnp.float32),
        ],
        cost_estimate=pl.CostEstimate(
            flops=2 * size**3, bytes_accessed=60 * size * size * 4, transcendentals=0
        ),
    )(gram)


def on_device(raw_panel, raw_trail, panel_shift, trail_shift):
    pcols = raw_panel.shape[0]
    pixels = raw_panel.shape[1]
    n = lax.axis_size("rows")
    my_row = lax.axis_index("rows")
    root = math.sqrt(pixels * n)
    depth = lax.axis_size("cols")
    trows = raw_trail.shape[0]
    panel, panel_mine = grouped(raw_panel, panel_shift, n, my_row, 1)
    trail, trail_mine = grouped(raw_trail, trail_shift, n, my_row, 2)
    full, front, moved = exchange(panel, trail, panel_mine, trail_mine, n, depth)
    full_panel = full.reshape(depth, -1, pixels)[:, :pcols].reshape(depth * pcols, pixels)
    full_panel = lax.optimization_barrier(full_panel)
    gram = sum_rows(inner_rows(full_panel, full_panel, lax.Precision.HIGHEST), n, 1)
    gram, moved = lax.optimization_barrier((gram, moved))
    rest = lax.all_to_all(moved, "rows", split_axis=0, concat_axis=0, tiled=True)
    reg_trail = jnp.concatenate([front, rest], axis=1).reshape(-1, pixels)[:trows]
    reg_trail = lax.optimization_barrier(reg_trail)
    r_factor, inverse = factor(gram, 1.0 / root)
    cross = sum_rows(inner_rows(full_panel, reg_trail, lax.Precision.HIGH), n, 2)
    highest = lax.Precision.HIGHEST
    coupling = jnp.dot(inverse, cross, precision=highest, preferred_element_type=jnp.float32)
    weights = lax.dot_general(
        inverse,
        coupling,
        (((0,), (0,)), ((), ())),
        precision=highest,
        preferred_element_type=jnp.float32,
    )
    removed = lax.dot_general(
        weights,
        full_panel,
        (((0,), (0,)), ((), ())),
        precision=lax.Precision.HIGH,
        preferred_element_type=jnp.float32,
    )
    trail_out = reg_trail - removed
    own = lax.dynamic_slice_in_dim(inverse, lax.axis_index("cols") * pcols, pcols, 0)
    q_panel = jnp.dot(
        own * root, full_panel, precision=lax.Precision.HIGH, preferred_element_type=jnp.float32
    )
    return (r_factor, coupling / root, q_panel, trail_out)


def solution(mesh):
    placed = (P("cols", "rows"), P("cols", "rows"), P("cols"), P("cols"))
    return jax.shard_map(
        on_device,
        mesh=mesh,
        in_specs=placed,
        out_specs=(P(), P(None, "cols"), P("cols", "rows"), P("cols", "rows")),
        check_vma=False,
    )
```

profile of v0, /device:TPU:9, one launch (start us, length us, event | category | flops | bytes accessed | tf_op | source)
XLA Modules:
  0.0 201.1 jit_solution(7507506265094147585)
XLA Ops:
  0.6 2.4 %copy.17 = f32[8,8,32,128]{3,2,1,0:T(8,128)} copy(f32[8,8,32,128]{3,1,2,0:T(8,128)} %bitcast.45) | data formatting | bytes 2097152
  3.0 5.0 %copy.9 = f32[32,8,32,128]{3,2,1,0:T(8,128)} copy(f32[32,8,32,128]{3,1,2,0:T(8,128)} %bitcast.41) | data formatting | bytes 8388608
  8.0 0.6 dynamic_slice.10.trail_shift
  8.6 0.6 dynamic_slice.9.panel_shift
  9.2 100.6 %shard_map.75 = (f32[4,64,32,128]{3,2,1,0:T(8,128)}, f32[8,16,32,128]{3,2,1,0:T(8,128)}, f32[8,16,32,128]{3,2,1,0:T(8,128)}) custom-call(s32[8]{0:T(128)} %dynamic_slice.9.panel_shift, s32[32]{0:T(128)} %dynamic_slice.10.trail_shift, f32[8,8,32,128]{3,2,1,0:T(8,128)} %copy.17, f32[8,32,32,128]{3,2,1,0:T(8,128)} %bitcast.39), custom_call_target="tpu_custom_call" | custom-call | bytes 167772160 | tf_op jit(solution)/shard_map/pallas_call | solution.py:243
  109.8 6.0 %copy.16 = f32[32,8,32,128]{3,1,2,0:T(8,128)S(1)} copy(f32[32,8,32,128]{3,2,1,0:T(8,128)} %bitcast.42) | data formatting | bytes 8388608
  115.8 0.0 copy-start
  115.8 4.2 %fusion.6 = f32[256,256]{1,0:T(8,128)} fusion(f32[256,4096]{1,0:T(8,128)S(1)} %bitcast.33), kind=kOutput, calls=%fused_computation.12 | convolution fusion | flops 3221225472 | bytes 4456448 | tf_op jit(solution)/shard_map/dot_general | solution.py:288
  120.0 0.0 copy-done
  120.0 13.0 %shard_map.76 = f32[8,32,256]{2,1,0:T(8,128)} custom-call(f32[8,32,256]{2,1,0:T(8,128)} %bitcast.43), custom_call_target="tpu_custom_call" | custom-call | bytes 4194304 | tf_op jit(solution)/shard_map/pallas_call | solution.py:347
  133.1 3.9 %all-to-all-start = ((f32[8,16,32,128]{3,2,1,0:T(8,128)}), f32[8,16,32,128]{3,2,1,0:T(8,128)S(1)}, u32[]{:S(2)}, u32[]{:S(2)}) async-start(f32[8,16,32,128]{3,2,1,0:T(8,128)} %get-tuple-element.17), calls=%async_computation | async-start | bytes 4194304 | tf_op jit(solution)/shard_map/all_to_all | solution.py:443
  136.9 26.9 %shard_map.77 = (f32[256,256]{1,0:T(8,128)}, f32[256,256]{1,0:T(8,128)}) custom-call(f32[256,256]{1,0:T(8,128)} %bitcast.46), custom_call_target="tpu_custom_call" | custom-call | flops 33554432 | bytes 15728640 | tf_op jit(solution)/shard_map/pallas_call | solution.py:413
  163.8 4.6 %fusion = f32[64,4096]{1,0:T(8,128)} fusion(f32[256,4096]{1,0:T(8,128)} %bitcast.34, f32[256,256]{1,0:T(8,128)} %get-tuple-element.15, s32[]{:T(128)S(6)} %select_n.11), kind=kOutput, calls=%fused_computation.6 | convolution fusion | flops 402669568 | bytes 5308420 | tf_op jit(solution)/shard_map/dot_general | solution.py:466
  168.4 0.0 all-to-all-done
  168.4 2.3 %pad_maximum_fusion = f32[8,32,32,128]{3,2,1,0:T(8,128)S(1)} fusion(f32[8,16,32,128]{3,2,1,0:T(8,128)S(1)} %all-to-all-done, f32[8,16,32,128]{3,2,1,0:T(8,128)} %get-tuple-element.16), kind=kLoop, calls=%fused_computation.3 | loop fusion | flops 1048576 | bytes 8388608 | tf_op jit(solution)/shard_map/concatenate | solution.py:444
  170.7 4.1 %copy.15 = f32[32,8,32,128]{3,1,2,0:T(8,128)S(1)} copy(f32[32,8,32,128]{3,2,1,0:T(8,128)S(1)} %bitcast.40) | data formatting | bytes 8388608
  174.7 0.0 copy-start.2
  174.8 0.0 copy-start.3
  174.8 2.6 %fusion.7 = f32[256,256]{1,0:T(8,128)} fusion(f32[256,4096]{1,0:T(8,128)S(1)} %bitcast.36, f32[256,4096]{1,0:T(8,128)S(1)} %bitcast.37), kind=kOutput, calls=%fused_computation.13 | convolution fusion | flops 1610612736 | bytes 8650752 | tf_op jit(solution)/shard_map/dot_general | solution.py:288
  177.4 0.0 copy-done.2
  177.4 13.5 %shard_map.78 = f32[8,32,256]{2,1,0:T(8,128)} custom-call(f32[8,32,256]{2,1,0:T(8,128)} %bitcast.44), custom_call_target="tpu_custom_call" | custom-call | bytes 4194304 | tf_op jit(solution)/shard_map/pallas_call | solution.py:347
  190.9 2.0 %broadcast_multiply_fusion = (f32[256,256]{1,0:T(8,128)}, f32[256,256]{1,0:T(8,128)S(1)}) fusion(f32[256,256]{1,0:T(8,128)S(1)} %copy-done.3, f32[256,256]{1,0:T(8,128)} %bitcast.47), kind=kOutput, calls=%fused_computation.5 | convolution fusion | flops 201392128 | bytes 1048576 | tf_op jit(solution)/shard_map/dot_general | solution.py:449
  193.0 0.6 fusion.8
  193.6 7.6 %convolution_subtract_fusion = f32[256,4096]{1,0:T(8,128)} fusion(f32[256,4096]{1,0:T(8,128)} %bitcast.38, f32[256,256]{1,0:T(8,128)S(1)} %fusion.8, f32[256,4096]{1,0:T(8,128)} %bitcast.35), kind=kOutput, calls=%fused_computation | convolution fusion | flops 1611661312 | bytes 12845056 | tf_op jit(solution)/shard_map/dot_general | solution.py:457
  (7 shorter events, 0.0 us)
Async XLA Ops:
  3.0 5.0 %copy-start.4 = (s32[256]{0:T(256)S(1)}, s32[256]{0:T(256)}, u32[]{:S(2)}) copy-start(s32[256]{0:T(256)} %param.7) | copy-start | bytes 3076
  3.0 5.6 %copy-start.5 = (s32[64]{0:T(128)S(1)}, s32[64]{0:T(128)}, u32[]{:S(2)}) copy-start(s32[64]{0:T(128)} %param.6) | copy-start | bytes 772
  115.8 4.3 %copy-start = (f32[32,8,32,128]{3,1,2,0:T(8,128)}, f32[32,8,32,128]{3,1,2,0:T(8,128)S(1)}, u32[]{:S(2)}) copy-start(f32[32,8,32,128]{3,1,2,0:T(8,128)S(1)} %copy.16) | copy-start | bytes 12582916
  133.1 35.3 %all-to-all-start = ((f32[8,16,32,128]{3,2,1,0:T(8,128)}), f32[8,16,32,128]{3,2,1,0:T(8,128)S(1)}, u32[]{:S(2)}, u32[]{:S(2)}) async-start(f32[8,16,32,128]{3,2,1,0:T(8,128)} %get-tuple-element.17), calls=%async_computation | async-start | bytes 4194304 | tf_op jit(solution)/shard_map/all_to_all | solution.py:443
  170.7 4.1 %copy-start.1 = (f32[32,8,32,128]{3,1,2,0:T(8,128)S(1)}, f32[32,8,32,128]{3,1,2,0:T(8,128)}, u32[]{:S(2)}) copy-start(f32[32,8,32,128]{3,1,2,0:T(8,128)} %copy-done) | copy-start | bytes 12582916
  174.7 2.7 %copy-start.2 = (f32[32,8,32,128]{3,1,2,0:T(8,128)}, f32[32,8,32,128]{3,1,2,0:T(8,128)S(1)}, u32[]{:S(2)}) copy-start(f32[32,8,32,128]{3,1,2,0:T(8,128)S(1)} %copy.15) | copy-start | bytes 12582916
  174.8 16.2 %copy-start.3 = (f32[256,256]{1,0:T(8,128)S(1)}, f32[256,256]{1,0:T(8,128)}, u32[]{:S(2)}) copy-start(f32[256,256]{1,0:T(8,128)} %get-tuple-element.15) | copy-start | bytes 786436
where the time goes:
time: 204 us; the launch traced here: 201 us
  Pallas kernels  154 us (75%)
  matrix products  21.7 us (11%)
  local copies, waits for them, and re-layouts  18.6 us (9%)
  starting transfers between devices  3.86 us (2%)
  other arithmetic  2.27 us (1%)
    pallas_call x1, Pallas kernels, exchange(): pl.pallas_call(functools.partial(exchange_kernel, n, depth, pieces, chunk...  101 us
    pallas_call x1, Pallas kernels, factor(): pl.pallas_call(functools.partial(factor_kernel, size, tile, scale), out_s...  26.9 us
    pallas_call x2, Pallas kernels, sum_rows(): pl.pallas_call(functools.partial(sum_kernel, n), out_shape=jax.ShapeDtype...  26.5 us
    unnamed x16, local copies, waits for them, and re-layouts  17.4 us
    dot_general x1, matrix products, on_device(): lax.dot_general(weights, full_panel, (((0,), (0,)), ((), ())), precision=...  7.56 us
    dot_general x2, matrix products, inner_rows(): lax.dot_general(left, right, (((1,), (1,)), ((), ())), precision=precisio...  6.87 us
    dot_general x1, matrix products, on_device(): jnp.dot(own * root, full_panel, precision=lax.Precision.HIGH, preferred_e...  4.59 us
  transfers between devices with their start and end apart: 1, of which 0 were waited for; matrix products, arithmetic and copies ran while one was open for 2% of the time, Pallas kernels for 13%

commit v1 on v0

v1 whole, which is shorter than its diff:
```python
import functools
import math

import jax
import jax.numpy as jnp
from jax import lax
from jax.experimental import pallas as pl
from jax.experimental.pallas import tpu as pltpu
from jax.sharding import PartitionSpec as P

BW = 128
SUB = 8
MESH = pl.DeviceIdType.MESH
F32 = jnp.float32
HIGHEST = lax.Precision.HIGHEST
HIGH = lax.Precision.HIGH


def rows_dot(left, right, precision):
    return lax.dot_general(
        left,
        right,
        (((1,), (1,)), ((), ())),
        precision=precision,
        preferred_element_type=F32,
    )


def plain_dot(left, right, precision):
    return lax.dot_general(
        left,
        right,
        (((1,), (0,)), ((), ())),
        precision=precision,
        preferred_element_type=F32,
    )


def only(cond, always):
    if always:
        return lambda fn: fn()
    return pl.when(cond)


def fused_kernel(
    n,
    depth,
    pieces,
    scale,
    panel_shift,
    trail_shift,
    panel,
    trail,
    full,
    reg,
    upper_ref,
    inv_ref,
    own_ref,
    cross_ref,
    ring_p,
    moved_p,
    moved_t,
    gram_part,
    gram_land,
    gram_sum,
    cross_part,
    cross_land,
    aug,
    pair,
    p1_send,
    p1_recv,
    p2_send,
    p2_recv,
    t1_send,
    t1_recv,
    t2_send,
    t2_recv,
    z_send,
    z_recv,
    g_send,
    g_recv,
    c_send,
    c_recv,
    f_send,
    f_recv,
    local_sem,
    *rings,
):
    me = lax.axis_index("rows")
    z = lax.axis_index("cols")
    ctp, blocks = panel.shape[0], panel.shape[1]
    ctt = trail.shape[0]
    total = n * blocks
    tp = ring_p.shape[0]
    tt = len(rings)
    op, ot = ctp // tp, ctt // tt
    rows_t = ot * SUB
    sr = cross_land.shape[2]
    oc = rows_t // sr
    size = inv_ref.shape[0]
    mid_lo = max(depth // 2 - 1, 0)
    mid_hi = min(depth // 2, depth - 1)
    mine = pl.ds(pl.multiple_of(me * blocks, blocks), blocks)

    def each_peer(fn):
        def body(d, carry):
            fn(d, lax.rem(me + d, n), lax.rem(me - d + n, n))
            return carry

        lax.fori_loop(1, n, body, 0)

    def linked(other):
        near = (z - other == 1) | (other - z == 1)
        low = ((z == mid_lo) & (other < mid_lo)) | ((z < mid_lo) & (other == mid_lo))
        high = ((z == mid_hi) & (other > mid_hi)) | ((z > mid_hi) & (other == mid_hi))
        return near | low | high

    barrier = pltpu.get_barrier_semaphore()
    for d in range(1, n):
        pl.semaphore_signal(
            barrier, inc=1, device_id={"rows": lax.rem(me + d, n)}, device_id_type=MESH
        )
    greeted = n - 1
    for other in range(depth):

        @pl.when(linked(other))
        def _():
            pl.semaphore_signal(barrier, inc=1, device_id={"cols": other}, device_id_type=MESH)

        greeted = greeted + jnp.where(linked(other), 1, 0)
    pl.semaphore_wait(barrier, greeted)

    def row_copy(src, dst, send, recv, to):
        return pltpu.make_async_remote_copy(
            src_ref=src,
            dst_ref=dst,
            send_sem=send,
            recv_sem=recv,
            device_id={"rows": to},
            device_id_type=MESH,
        )

    def p1(d, to):
        return row_copy(
            panel.at[pl.ds(to * tp, tp)],
            ring_p.at[:, mine],
            p1_send.at[d - 1],
            p1_recv.at[d - 1],
            to,
        )

    def p2(d, to):
        return row_copy(
            moved_p.at[to],
            full.at[z, pl.ds(me * tp, tp)],
            p2_send.at[d - 1],
            p2_recv.at[d - 1],
            to,
        )

    def t1(t, d, to):
        return row_copy(
            trail.at[to * tt + t],
            rings[t].at[mine],
            t1_send.at[t, d - 1],
            t1_recv.at[t, d - 1],
            to,
        )

    def t2(t, d, to):
        return row_copy(
            moved_t.at[t, to],
            reg.at[me, t],
            t2_send.at[t, d - 1],
            t2_recv.at[t, d - 1],
            to,
        )

    own_p = pltpu.make_async_copy(
        panel.at[pl.ds(me * tp, tp)], ring_p.at[:, mine], local_sem.at[0]
    )

    def own_t(t):
        return pltpu.make_async_copy(
            trail.at[me * tt + t], rings[t].at[mine], local_sem.at[1 + t]
        )

    def started(copies, active, count):
        def go(d, to, origin):
            @only(active(to), count == n)
            def _():
                copies(d, to).start()

        each_peer(go)

    def landed(copies, active, count, by_origin):
        def go(d, to, origin):
            @only(active(origin if by_origin else me), count == n)
            def _():
                copies(d, to).wait_recv()

        each_peer(go)

    def left(copies, active, count, by_target):
        def go(d, to, origin):
            @only(active(to if by_target else me), count == n)
            def _():
                copies(d, to).wait_send()

        each_peer(go)

    def has_p(j):
        return j < op

    def has_t(j):
        return j < ot

    sub = lax.broadcasted_iota(jnp.int32, (1, SUB, BW), 1)
    step = min(16, blocks)

    def compose(ring, shifts, to, put):
        starts = [lax.rem(to * blocks - s + total, total) for s in shifts]
        for h in range(0, blocks, step):
            block = ring[pl.ds(starts[0] + h, step)]
            for c in range(1, SUB):
                block = jnp.where(sub == c, ring[pl.ds(starts[c] + h, step)], block)
            put(h, block)

    def wrap(ring):
        ring[pl.ds(total, blocks)] = ring[pl.ds(0, blocks)]

    def line(side, d, q):
        step_z = 1 if side == 0 else -1
        origin = z - step_z * (d - 1)
        rows = pl.ds(q * (ctp // pieces), ctp // pieces)
        return pltpu.make_async_remote_copy(
            src_ref=full.at[origin, rows],
            dst_ref=full.at[origin, rows],
            send_sem=z_send.at[side, d - 1, q],
            recv_sem=z_recv.at[side, d - 1, q],
            device_id={"cols": z + step_z},
            device_id_type=MESH,
        )

    def sends(side, d):
        if side == 0:
            return (z + 1 < depth) & (z - (d - 1) >= 0)
        return (z >= 1) & (z + (d - 1) < depth)

    def receives(side, d):
        return z - d >= 0 if side == 0 else z + d < depth

    def arrived(side, d, q):
        step_z = 1 if side == 0 else -1
        origin = z - step_z * d
        rows = pl.ds(q * (ctp // pieces), ctp // pieces)
        return pltpu.make_async_remote_copy(
            src_ref=full.at[origin, rows],
            dst_ref=full.at[origin, rows],
            send_sem=z_send.at[side, d - 1, q],
            recv_sem=z_recv.at[side, d - 1, q],
            device_id={"cols": z - step_z},
            device_id_type=MESH,
        )

    def forward(d):
        for q in range(pieces):
            for side in (0, 1):

                @pl.when(receives(side, d))
                def _():
                    arrived(side, d, q).wait_recv()

                if d + 1 < depth:

                    @pl.when(sends(side, d + 1))
                    def _():
                        line(side, d + 1, q).start()

    def start_t1(t):
        @only(has_t(me), ot == n)
        def _():
            own_t(t).start()

        started(functools.partial(t1, t), has_t, ot)

    def turn_t(t):
        @only(has_t(me), ot == n)
        def _():
            own_t(t).wait()

        landed(functools.partial(t1, t), has_t, ot, False)

        @only(has_t(me), ot == n)
        def _():
            wrap(rings[t])
            shifts = [trail_shift[(me * tt + t) * SUB + c] for c in range(SUB)]

            def turn(d, to, origin):
                def put(h, block):
                    moved_t[t, to, pl.ds(h, step)] = block

                compose(rings[t], shifts, to, put)

            each_peer(turn)

            def keep(h, block):
                reg[me, t, pl.ds(h, step)] = block

            compose(rings[t], shifts, me, keep)

    def start_t2(t):
        def go(d, to, origin):
            t2(t, d, to).start()

        @only(has_t(me), ot == n)
        def _():
            each_peer(go)

    def wait_t2(t):
        landed(functools.partial(t2, t), has_t, ot, True)

    def panel_pair(b):
        cut = [full[:, :, 2 * b + k].reshape(size, BW) for k in range(2)]
        return jnp.concatenate(cut, axis=1)

    def make_gram():
        gram_part[...] = jnp.zeros_like(gram_part)

        def body(b, carry):
            block = panel_pair(b)
            gram_part[...] += rows_dot(block, block, HIGHEST).reshape(gram_part.shape)
            return carry

        lax.fori_loop(0, blocks // 2, body, 0)

    def g_one(d, to):
        return row_copy(
            gram_part.at[to], gram_land.at[d - 1], g_send.at[0, d - 1], g_recv.at[0, d - 1], to
        )

    def g_two(d, to):
        return row_copy(
            gram_sum.at[me], gram_sum.at[me], g_send.at[1, d - 1], g_recv.at[1, d - 1], to
        )

    def every(j):
        return j >= 0

    def has_c(j):
        return j < oc

    def make_cross(t):
        cross_part[t] = jnp.zeros_like(cross_part[t])

        def body(b, carry):
            cut = [reg[:, t, 2 * b + k].reshape(rows_t, BW) for k in range(2)]
            block = jnp.concatenate(cut, axis=1)
            cross_part[t] += rows_dot(block, panel_pair(b), HIGH).reshape(oc, sr, size)
            return carry

        lax.fori_loop(0, blocks // 2, body, 0)

    def c_one(t, d, to):
        return row_copy(
            cross_part.at[t, to],
            cross_land.at[t, d - 1],
            c_send.at[0, t, d - 1],
            c_recv.at[0, t, d - 1],
            to,
        )

    def c_two(t, d, to):
        return row_copy(
            cross_ref.at[t, me],
            cross_ref.at[t, me],
            c_send.at[1, t, d - 1],
            c_recv.at[1, t, d - 1],
            to,
        )

    def cross_scatter(t):
        started(functools.partial(c_one, t), has_c, oc)

    def cross_spread(t):
        @only(has_c(me), oc == n)
        def _():
            total_c = cross_part[t, me]
            for d in range(1, n):
                c_one(t, d, lax.rem(me + d, n)).wait_recv()
                total_c = total_c + cross_land[t, d - 1]
            cross_ref[t, me] = total_c

            def go(d, to, origin):
                c_two(t, d, to).start()

            each_peer(go)

    def cross_done(t):
        landed(functools.partial(c_two, t), has_c, oc, True)

    tile = min(64, size)
    tiles = size // tile
    low_count = mid_lo
    high_count = depth - 1 - mid_hi

    def factor_copy(i, k, slot, to):
        ref = inv_ref if k == 0 else upper_ref
        rows = pl.ds(i * tile, tile)
        return pltpu.make_async_remote_copy(
            src_ref=ref.at[rows],
            dst_ref=ref.at[rows],
            send_sem=f_send.at[slot, i, k],
            recv_sem=f_recv.at[i, k],
            device_id={"cols": to},
            device_id_type=MESH,
        )

    def factor_sends(act):
        for k in (0, 1):
            for i in range(tiles):
                send_factor(i, k, act)

    def send_factor(i, k, act):
        for slot in range(low_count):

            @pl.when(z == mid_lo)
            def _():
                act(factor_copy(i, k, slot, slot))

        for slot in range(high_count):

            @pl.when(z == mid_hi)
            def _():
                act(factor_copy(i, k, slot, mid_hi + 1 + slot))

    def factor_tile(i):
        lo = i * tile
        hi = lo + tile
        row = lax.broadcasted_iota(jnp.int32, (tile, 2 * tile), 0)
        col = lax.broadcasted_iota(jnp.int32, (tile, 2 * tile), 1)
        pair[...] = jnp.where(col == row + tile, 1.0, 0.0)
        pair[:, 0:tile] = aug[lo:hi, lo:hi]
        w = pair[...]
        pivots = jnp.zeros((tile, 1), F32)
        for j in range(tile):
            base = j // 8 * 8
            live = w[base:, :]
            lead = w[j : j + 1, :]
            pivot = lead[:, j : j + 1]
            pivots = jnp.where(row[:, 0:1] == j, pivot, pivots)
            if j + 1 == tile:
                break
            mult = jnp.where(row[base:, 0:1] > j, live[:, j : j + 1], 0.0)
            live = live - mult * (lead / pivot)
            w = live if base == 0 else jnp.concatenate([w[:base], live], axis=0)
        pair[...] = w * (1.0 / jnp.sqrt(pivots))
        inverse = pair[:, tile : 2 * tile]
        lead_rows = plain_dot(inverse, aug[lo:hi, :], HIGHEST)
        grow = lax.broadcasted_iota(jnp.int32, (tile, size), 0) + lo
        gcol = lax.broadcasted_iota(jnp.int32, (tile, size), 1)
        upper = jnp.where(gcol >= grow, lead_rows[:, 0:size], 0.0)
        upper_ref[lo:hi, :] = upper * scale
        inv_ref[lo:hi, :] = lead_rows[:, size : 2 * size]
        if hi < size:
            aug[...] = aug[...] - lax.dot_general(
                upper,
                lead_rows,
                (((0,), (0,)), ((), ())),
                precision=HIGHEST,
                preferred_element_type=F32,
            )

    def start_copy(copy):
        copy.start()

    @only(has_p(me), op == n)
    def _():
        own_p.start()

    started(p1, has_p, op)

    @only(has_p(me), op == n)
    def _():
        own_p.wait()

    landed(p1, has_p, op, False)

    @only(has_p(me), op == n)
    def _():
        for t in range(tp):
            wrap(ring_p.at[t])
        shifts = [
            [panel_shift[(me * tp + t) * SUB + c] for c in range(SUB)] for t in range(tp)
        ]

        def turn(d, to, origin):
            for t in range(tp):

                def put(h, block, t=t):
                    moved_p[to, t, pl.ds(h, step)] = block

                compose(ring_p.at[t], shifts[t], to, put)

        each_peer(turn)

        def go(d, to, origin):
            p2(d, to).start()

        each_peer(go)
        for t in range(tp):

            def keep(h, block, t=t):
                full[z, me * tp + t, pl.ds(h, step)] = block

            compose(ring_p.at[t], shifts[t], me, keep)

    last = tt - 1
    start_t1(0)
    if tt > 1:
        start_t1(1)
    landed(p2, has_p, op, True)
    for q in range(pieces):
        for side in (0, 1):

            @pl.when(sends(side, 1))
            def _():
                line(side, 1, q).start()

    middle = max(depth // 2, 1)
    turn_t(0)
    if last > 0:
        start_t2(0)
    for t in range(2, last):
        start_t1(t)
    if depth > 1:
        forward(1)
    for t in range(1, last):
        turn_t(t)
        if t + 1 < last:
            start_t2(t)
        if t == 1:
            for d in range(2, middle + 1):
                forward(d)
    if last < 2:
        for d in range(2, middle + 1):
            forward(d)

    def rest_t1():
        if last > 1:
            start_t1(last)

    def rest_t2():
        if last > 1:
            start_t2(last - 1)

    def finish_turns():
        if last > 0:
            turn_t(last)
        start_t2(last)

    central = (z == mid_lo) | (z == mid_hi)

    @pl.when(central)
    def _():
        make_gram()
        started(g_one, every, n)
        aug_row = lax.broadcasted_iota(jnp.int32, (size, size), 0)
        aug_col = lax.broadcasted_iota(jnp.int32, (size, size), 1)
        aug[:, size : 2 * size] = jnp.where(aug_row == aug_col, 1.0, 0.0)
        total_g = gram_part[me]
        for d in range(1, n):
            g_one(d, lax.rem(me + d, n)).wait_recv()
            total_g = total_g + gram_land[d - 1]
        gram_sum[me] = total_g
        started(g_two, every, n)
        rest_t1()
        rest_t2()
        landed(g_two, every, n, True)
        aug[:, 0:size] = gram_sum[...].reshape(size, size)
        for i in range(tiles):
            factor_tile(i)
            send_factor(i, 0, start_copy)
            if i == min(1, tiles - 1):
                finish_turns()
        for i in range(tiles):
            send_factor(i, 1, start_copy)
        left(g_one, every, n, True)
        left(g_two, every, n, True)

    @pl.when(jnp.logical_not(central))
    def _():
        rest_t1()
        rest_t2()
        for d in range(middle + 1, depth):
            forward(d)
        finish_turns()

    for t in range(last):
        wait_t2(t)
        make_cross(t)
        cross_scatter(t)
    for t in range(last):
        cross_spread(t)
    wait_t2(last)
    make_cross(last)
    cross_scatter(last)
    cross_spread(last)

    @pl.when(jnp.logical_not(central))
    def _():
        for i in range(tiles):
            for k in (0, 1):
                factor_copy(i, k, 0, mid_lo).wait_recv()

    own = inv_ref.shape[0] // depth
    own_ref[...] = inv_ref[pl.ds(pl.multiple_of(z * own, own), own), :]
    for t in range(tt):
        cross_done(t)

    @pl.when(central)
    def _():
        factor_sends(lambda copy: copy.wait_send())

    left(p1, has_p, op, True)
    left(p2, has_p, op, False)
    for t in range(tt):
        left(functools.partial(t1, t), has_t, ot, True)
        left(functools.partial(t2, t), has_t, ot, False)
        left(functools.partial(c_one, t), has_c, oc, True)
        left(functools.partial(c_two, t), has_c, oc, False)
    for d in range(1, depth):
        for q in range(pieces):
            for side in (0, 1):

                @pl.when(sends(side, d))
                def _():
                    line(side, d, q).wait_send()


def fused(panel, trail, panel_shift, trail_shift, n, depth, scale):
    ctp, blocks = panel.shape[0], panel.shape[1]
    ctt = trail.shape[0]
    tp = -(-ctp // n)
    tt = -(-ctt // n)
    op, ot = ctp // tp, ctt // tt
    size = depth * ctp * SUB
    rows_t = ot * SUB
    sr = max(SUB, rows_t // n)
    oc = rows_t // sr
    tiles = max(size // 64, 1)
    pieces = 4 if ctp % 4 == 0 else 1
    total = n * blocks
    smem = pl.BlockSpec(memory_space=pltpu.SMEM)
    vmem = pl.BlockSpec(memory_space=pltpu.VMEM)
    hbm = pl.BlockSpec(memory_space=pl.ANY)
    dma = pltpu.SemaphoreType.DMA
    peers = max(n - 1, 1)
    lines = max(depth - 1, 1)
    square = jax.ShapeDtypeStruct((size, size), F32)
    return pl.pallas_call(
        functools.partial(fused_kernel, n, depth, pieces, scale),
        out_shape=(
            jax.ShapeDtypeStruct((depth, ctp, blocks, SUB, BW), F32),
            jax.ShapeDtypeStruct((ot, tt, blocks, SUB, BW), F32),
            square,
            square,
            jax.ShapeDtypeStruct((size // depth, size), F32),
            jax.ShapeDtypeStruct((tt, oc, sr, size), F32),
        ),
        in_specs=[smem, smem, hbm, hbm],
        out_specs=(vmem,) * 6,
        scratch_shapes=[
            pltpu.VMEM((tp, total + blocks, SUB, BW), F32),
            pltpu.VMEM((n, tp, blocks, SUB, BW), F32),
            pltpu.VMEM((tt, n, blocks, SUB, BW), F32),
            pltpu.VMEM((n, size // n, size), F32),
            pltpu.VMEM((peers, size // n, size), F32),
            pltpu.VMEM((n, size // n, size), F32),
            pltpu.VMEM((tt, oc, sr, size), F32),
            pltpu.VMEM((tt, peers, sr, size), F32),
            pltpu.VMEM((size, 2 * size), F32),
            pltpu.VMEM((size // tiles, 2 * (size // tiles)), F32),
            dma((peers,)),
            dma((peers,)),
            dma((peers,)),
            dma((peers,)),
            dma((tt, peers)),
            dma((tt, peers)),
            dma((tt, peers)),
            dma((tt, peers)),
            dma((2, lines, pieces)),
            dma((2, lines, pieces)),
            dma((2, peers)),
            dma((2, peers)),
            dma((2, tt, peers)),
            dma((2, tt, peers)),
            dma((lines, tiles, 2)),
            dma((tiles, 2)),
            dma((1 + tt,)),
        ]
        + [pltpu.VMEM((total + blocks, SUB, BW), F32)] * tt,
        compiler_params=pltpu.CompilerParams(collective_id=3, has_side_effects=True),
        cost_estimate=pl.CostEstimate(
            flops=0, bytes_accessed=40 * trail.size * 4, transcendentals=0
        ),
    )(panel_shift, trail_shift, panel, trail)


def final_kernel(
    root, full, reg, upper, inv, own, cross, r_ref, coupling_ref, q_ref, out_ref, weights
):
    size = inv.shape[0]
    ot, tt = reg.shape[0], reg.shape[1]
    part = full.shape[2]

    @pl.when(pl.program_id(0) == 0)
    def _():
        r_ref[...] = upper[...]
        for t in range(tt):
            rows = cross[t].reshape(ot * SUB, size)
            turned = rows_dot(rows, inv[...], HIGHEST)
            coupling_ref[:, t] = (turned * (1.0 / root)).reshape(ot, SUB, size)
            weights[:, t] = plain_dot(turned, inv[...], HIGHEST).reshape(ot, SUB, size)

    block = jnp.concatenate(
        [full[:, :, k].reshape(size, BW) for k in range(part)], axis=1
    )
    both = plain_dot(weights[...].reshape(ot * tt * SUB, size), block, HIGH)
    basis = plain_dot(own[...] * root, block, HIGH)
    for k in range(part):
        lanes = slice(k * BW, (k + 1) * BW)
        out_ref[:, :, k] = reg[:, :, k] - both[:, lanes].reshape(ot, tt, SUB, BW)
        q_ref[:, k] = basis[:, lanes].reshape(q_ref.shape[0], SUB, BW)


def final(full, reg, upper, inv, own, cross, root):
    depth, ctp, blocks = full.shape[:3]
    ot, tt = reg.shape[:2]
    size = inv.shape[0]
    part = 4 if blocks % 4 == 0 else 1
    whole = lambda shape: pl.BlockSpec(shape, lambda i: (0,) * len(shape))
    reg_spec = pl.BlockSpec((ot, tt, part, SUB, BW), lambda i: (0, 0, i, 0, 0))
    return pl.pallas_call(
        functools.partial(final_kernel, root),
        grid=(blocks // part,),
        out_shape=(
            jax.ShapeDtypeStruct((size, size), F32),
            jax.ShapeDtypeStruct((ot, tt, SUB, size), F32),
            jax.ShapeDtypeStruct((ctp, blocks, SUB, BW), F32),
            jax.ShapeDtypeStruct((ot, tt, blocks, SUB, BW), F32),
        ),
        in_specs=[
            pl.BlockSpec((depth, ctp, part, SUB, BW), lambda i: (0, 0, i, 0, 0)),
            reg_spec,
            whole((size, size)),
            whole((size, size)),
            whole((size // depth, size)),
            whole(cross.shape),
        ],
        out_specs=(
            whole((size, size)),
            whole((ot, tt, SUB, size)),
            pl.BlockSpec((ctp, part, SUB, BW), lambda i: (0, i, 0, 0)),
            reg_spec,
        ),
        scratch_shapes=[pltpu.VMEM((ot, tt, SUB, size), F32)],
        cost_estimate=pl.CostEstimate(
            flops=2 * size * (reg.size + full.size), bytes_accessed=12 * reg.size, transcendentals=0
        ),
    )(full, reg, upper, inv, own, cross)


def tiled(raw):
    rows, pixels = raw.shape
    return raw.reshape(rows // SUB, SUB, pixels // BW, BW).transpose(0, 2, 1, 3)


def flat(blocked):
    cut, blocks = blocked.shape[0], blocked.shape[1]
    return blocked.transpose(0, 2, 1, 3).reshape(cut * SUB, blocks * BW)


def on_device(raw_panel, raw_trail, panel_shift, trail_shift):
    n = lax.axis_size("rows")
    depth = lax.axis_size("cols")
    pixels = raw_panel.shape[1]
    root = math.sqrt(pixels * n)
    full, reg, upper, inv, own, cross = fused(
        tiled(raw_panel), tiled(raw_trail), panel_shift, trail_shift, n, depth, 1.0 / root
    )
    r_factor, coupling, q_panel, out = final(full, reg, upper, inv, own, cross, root)
    coupling = coupling.reshape(-1, coupling.shape[-1]).T
    out = flat(out.reshape((-1,) + out.shape[2:]))
    return (r_factor, coupling, flat(q_panel), out)


def solution(mesh):
    placed = (P("cols", "rows"), P("cols", "rows"), P("cols"), P("cols"))
    return jax.shard_map(
        on_device,
        mesh=mesh,
        in_specs=placed,
        out_specs=(P(), P(None, "cols"), P("cols", "rows"), P("cols", "rows")),
        check_vma=False,
    )
```

time: 204 us -> 174 us (0.85); the launches traced: 201 us -> 174 us
  matrix products: 21.7 us -> 0 us
  Pallas kernels: 154 us -> 172 us
  local copies, waits for them, and re-layouts: 18.6 us -> 1.79 us
  starting transfers between devices: 3.86 us -> 0 us
  other arithmetic: 2.27 us -> 0 us
    dot_general x6 -> x0, matrix products: 21.7 us -> none  [the longest x1 7.56 us: on_device(): lax.dot_general(weights, full_panel, (((0,), (0,)), ((), ())), precision=...]
    pallas_call x4 -> x2, Pallas kernels: 154 us -> 172 us  [the longest x1 159 us: fused(): pl.pallas_call(functools.partial(fused_kernel, n, depth, pieces, scale),...]
    unnamed x16 -> x0, local copies, waits for them, and re-layouts: 17.4 us -> none
    all_to_all x1 -> x0, starting transfers between devices: 3.86 us -> none  [on_device(): lax.all_to_all(moved, 'rows', split_axis=0, concat_axis=0, tiled=True)]
    concatenate x1 -> x0, other arithmetic: 2.27 us -> none  [on_device(): jnp.concatenate([front, rest], axis=1).reshape(-1, pixels)[:trows]]
  transfers between devices with their start and end apart: 1 -> 0, of which waited for: 0 -> 0; matrix products, arithmetic and copies ran while one was open for 2% -> 0% of each run, Pallas kernels for 13% -> 0%
where the time goes in v1:
time: 174 us
  Pallas kernels  172 us (99%)
  local copies, waits for them, and re-layouts  1.79 us (1%)
    pallas_call x1, Pallas kernels, fused(): pl.pallas_call(functools.partial(fused_kernel, n, depth, pieces, scale),...  159 us
    pallas_call x1, Pallas kernels, final(): pl.pallas_call(functools.partial(final_kernel, root), grid=(blocks // par...  12.5 us

profile of v1, /device:TPU:9, one launch (start us, length us, event | category | flops | bytes accessed | tf_op | source)
XLA Modules:
  0.0 174.0 jit_solution(9449807434174294226)
XLA Ops:
  0.6 159.1 %shard_map.75 = (f32[4,8,32,8,128]{4,3,2,1,0:T(8,128)}, f32[8,4,32,8,128]{4,3,2,1,0:T(8,128)}, f32[256,256]{1,0:T(8,128)}, f32[256,256]{1,0:T(8,128)}, f32[64,256]{1,0:T(8,128)}, /*index=5*/f32[4,8,8,256]{3,2,1,0:T(8,128)}) custom-call(s32[64]{0:T(128)} %panel_shift.1, s32[256]{0:T(256)} %trail_shift.1, f32[8,32,8,128]{3,2,1,0:T(8,128)} %bitcast.17, ...), custom_call_target="tpu_custom_call" | custom-call | bytes 167772160 | tf_op jit(solution)/shard_map/pallas_call | solution.py:661
  159.8 12.5 %shard_map.76 = (f32[256,256]{1,0:T(8,128)}, f32[8,4,8,256]{3,2,1,0:T(8,128)}, f32[8,32,8,128]{3,2,1,0:T(8,128)}, f32[8,4,32,8,128]{4,3,2,1,0:T(8,128)}) custom-call(f32[4,8,32,8,128]{4,3,2,1,0:T(8,128)} %get-tuple-element.14.full, f32[8,4,32,8,128]{4,3,2,1,0:T(8,128)} %get-tuple-element.15.reg, f32[256,256]{1,0:T(8,128)} %get-tuple-element.16.upper, ...), custom_call_target="tpu_custom_call" | custom-call | flops 1073741824 | bytes 12582912 | tf_op jit(solution)/shard_map/pallas_call | solution.py:744
  172.2 1.8 %copy.8 = f32[256,256]{0,1:T(8,128)} copy(f32[256,256]{1,0:T(8,128)} %bitcast.18) | data formatting | bytes 524288 | tf_op jit(solution)/shard_map/reshape | solution.py:793

commit v2 on v1

--- a/solution.py
+++ b/solution.py
@@ -36,6 +36,22 @@
     )
 
 
+def joined(parts):
+    return jnp.concatenate(parts, axis=0) if len(parts) > 1 else parts[0]
+
+
+def three_part(value):
+    high = value.astype(jnp.bfloat16)
+    low = (value - high.astype(F32)).astype(jnp.bfloat16)
+    return jnp.concatenate([high, high, low], axis=1)
+
+
+def removed(left_side, high_ref, low_ref, first, count):
+    high = jnp.concatenate([high_ref[first + k] for k in range(count)], axis=1)
+    low = jnp.concatenate([low_ref[first + k] for k in range(count)], axis=1)
+    return plain_dot(left_side, jnp.concatenate([high, low, high], axis=0), None)
+
+
 def only(cond, always):
     if always:
         return lambda fn: fn()
@@ -46,17 +62,19 @@
     n,
     depth,
     pieces,
-    scale,
+    root,
     panel_shift,
     trail_shift,
     panel,
     trail,
-    full,
-    reg,
     upper_ref,
     inv_ref,
-    own_ref,
     cross_ref,
+    q_ref,
+    reg,
+    high_ref,
+    low_ref,
+    full,
     ring_p,
     moved_p,
     moved_t,
@@ -320,19 +338,22 @@
     def wait_t2(t):
         landed(functools.partial(t2, t), has_t, ot, True)
 
-    def panel_pair(b):
-        cut = [full[:, :, 2 * b + k].reshape(size, BW) for k in range(2)]
+    def panel_block(b, count):
+        cut = [full[:, :, count * b + k].reshape(size, BW) for k in range(count)]
         return jnp.concatenate(cut, axis=1)
+
+    narrow = min(4, blocks)
+    wide = min(8, blocks)
 
     def make_gram():
         gram_part[...] = jnp.zeros_like(gram_part)
 
         def body(b, carry):
-            block = panel_pair(b)
+            block = panel_block(b, narrow)
             gram_part[...] += rows_dot(block, block, HIGHEST).reshape(gram_part.shape)
             return carry
 
-        lax.fori_loop(0, blocks // 2, body, 0)
+        lax.fori_loop(0, blocks // narrow, body, 0)
 
     def g_one(d, to):
         return row_copy(
@@ -354,12 +375,13 @@
         cross_part[t] = jnp.zeros_like(cross_part[t])
 
         def body(b, carry):
-            cut = [reg[:, t, 2 * b + k].reshape(rows_t, BW) for k in range(2)]
+            cut = [reg[:, t, wide * b + k].reshape(rows_t, BW) for k in range(wide)]
             block = jnp.concatenate(cut, axis=1)
-            cross_part[t] += rows_dot(block, panel_pair(b), HIGH).reshape(oc, sr, size)
+            both = rows_dot(block, panel_block(b, wide), HIGH)
+            cross_part[t] += both.reshape(oc, sr, size)
             return carry
 
-        lax.fori_loop(0, blocks // 2, body, 0)
+        lax.fori_loop(0, blocks // wide, body, 0)
 
     def c_one(t, d, to):
         return row_copy(
@@ -460,7 +482,7 @@
         grow = lax.broadcasted_iota(jnp.int32, (tile, size), 0) + lo
         gcol = lax.broadcasted_iota(jnp.int32, (tile, size), 1)
         upper = jnp.where(gcol >= grow, lead_rows[:, 0:size], 0.0)
-        upper_ref[lo:hi, :] = upper * scale
+        upper_ref[lo:hi, :] = upper * (1.0 / root)
         inv_ref[lo:hi, :] = lead_rows[:, size : 2 * size]
         if hi < size:
             aug[...] = aug[...] - lax.dot_general(
@@ -470,6 +492,43 @@
                 precision=HIGHEST,
                 preferred_element_type=F32,
             )
+
+    def make_basis():
+        factor = inv_ref[...]
+        own = pl.ds(pl.multiple_of(z * (ctp * SUB), ctp * SUB), ctp * SUB)
+
+        def body(b, carry):
+            both = plain_dot(factor, panel_block(b, narrow), HIGH)
+            mine_only = plain_dot(inv_ref[own, :] * root, panel_block(b, narrow), HIGH)
+            for k in range(narrow):
+                lanes = slice(k * BW, (k + 1) * BW)
+                place = narrow * b + k
+                part = both[:, lanes]
+                upper_half = part.astype(jnp.bfloat16)
+                high_ref[place] = upper_half
+                low_ref[place] = (part - upper_half.astype(F32)).astype(jnp.bfloat16)
+                q_ref[:, place] = mine_only[:, lanes].reshape(ctp, SUB, BW)
+            return carry
+
+        lax.fori_loop(0, blocks // narrow, body, 0)
+
+    def emit(chunks):
+        for t in chunks:
+            cross_done(t)
+        rows = [cross_ref[t].reshape(rows_t, size) for t in chunks]
+        left_side = three_part(rows_dot(joined(rows), inv_ref[...], HIGHEST))
+
+        def body(b, carry):
+            both = removed(left_side, high_ref, low_ref, narrow * b, narrow)
+            for k in range(narrow):
+                lanes = slice(k * BW, (k + 1) * BW)
+                place = narrow * b + k
+                for i, t in enumerate(chunks):
+                    part = both[i * rows_t : (i + 1) * rows_t, lanes]
+                    reg[:, t, place] = reg[:, t, place] - part.reshape(ot, SUB, BW)
+            return carry
+
+        lax.fori_loop(0, blocks // narrow, body, 0)
 
     def start_copy(copy):
         copy.start()
@@ -561,6 +620,13 @@
 
     central = (z == mid_lo) | (z == mid_hi)
 
+    def cross_chunk(t):
+        wait_t2(t)
+        make_cross(t)
+        cross_scatter(t)
+
+    early = min(2, last)
+
     @pl.when(central)
     def _():
         make_gram()
@@ -568,6 +634,8 @@
         aug_row = lax.broadcasted_iota(jnp.int32, (size, size), 0)
         aug_col = lax.broadcasted_iota(jnp.int32, (size, size), 1)
         aug[:, size : 2 * size] = jnp.where(aug_row == aug_col, 1.0, 0.0)
+        if early > 0:
+            cross_chunk(0)
         total_g = gram_part[me]
         for d in range(1, n):
             g_one(d, lax.rem(me + d, n)).wait_recv()
@@ -576,6 +644,8 @@
         started(g_two, every, n)
         rest_t1()
         rest_t2()
+        if early > 1:
+            cross_chunk(1)
         landed(g_two, every, n, True)
         aug[:, 0:size] = gram_sum[...].reshape(size, size)
         for i in range(tiles):
@@ -585,6 +655,10 @@
                 finish_turns()
         for i in range(tiles):
             send_factor(i, 1, start_copy)
+        for t in range(early):
+            cross_spread(t)
+        for t in range(early, last):
+            cross_chunk(t)
         left(g_one, every, n, True)
         left(g_two, every, n, True)
 
@@ -595,28 +669,30 @@
         for d in range(middle + 1, depth):
             forward(d)
         finish_turns()
-
-    for t in range(last):
-        wait_t2(t)
-        make_cross(t)
-        cross_scatter(t)
-    for t in range(last):
-        cross_spread(t)
-    wait_t2(last)
-    make_cross(last)
-    cross_scatter(last)
-    cross_spread(last)
+        for t in range(last):
+            cross_chunk(t)
+        for t in range(early):
+            cross_spread(t)
+
+    cross_chunk(last)
 
     @pl.when(jnp.logical_not(central))
     def _():
         for i in range(tiles):
-            for k in (0, 1):
-                factor_copy(i, k, 0, mid_lo).wait_recv()
-
-    own = inv_ref.shape[0] // depth
-    own_ref[...] = inv_ref[pl.ds(pl.multiple_of(z * own, own), own), :]
-    for t in range(tt):
+            factor_copy(i, 0, 0, mid_lo).wait_recv()
+
+    make_basis()
+    for t in range(early, tt):
+        cross_spread(t)
+    if early > 0:
+        emit(list(range(early)))
+    for t in range(early, tt):
         cross_done(t)
+
+    @pl.when(jnp.logical_not(central))
+    def _():
+        for i in range(tiles):
+            factor_copy(i, 1, 0, mid_lo).wait_recv()
 
     @pl.when(central)
     def _():
@@ -638,7 +714,7 @@
                     line(side, d, q).wait_send()
 
 
-def fused(panel, trail, panel_shift, trail_shift, n, depth, scale):
+def fused(panel, trail, panel_shift, trail_shift, n, depth, root):
     ctp, blocks = panel.shape[0], panel.shape[1]
     ctt = trail.shape[0]
     tp = -(-ctp // n)
@@ -657,20 +733,21 @@
     dma = pltpu.SemaphoreType.DMA
     peers = max(n - 1, 1)
     lines = max(depth - 1, 1)
-    square = jax.ShapeDtypeStruct((size, size), F32)
     return pl.pallas_call(
-        functools.partial(fused_kernel, n, depth, pieces, scale),
+        functools.partial(fused_kernel, n, depth, pieces, root),
         out_shape=(
-            jax.ShapeDtypeStruct((depth, ctp, blocks, SUB, BW), F32),
-            jax.ShapeDtypeStruct((ot, tt, blocks, SUB, BW), F32),
-            square,
-            square,
-            jax.ShapeDtypeStruct((size // depth, size), F32),
-            jax.ShapeDtypeStruct((tt, oc, sr, size), F32),
+            pltpu.VMEM((size, size), F32),
+            pltpu.VMEM((size, size), F32),
+            pltpu.VMEM((tt, oc, sr, size), F32),
+            pltpu.VMEM(panel.shape, F32),
+            pltpu.VMEM((ot, tt) + trail.shape[1:], F32),
+            pltpu.VMEM((blocks, size, BW), jnp.bfloat16),
+            pltpu.VMEM((blocks, size, BW), jnp.bfloat16),
         ),
         in_specs=[smem, smem, hbm, hbm],
-        out_specs=(vmem,) * 6,
+        out_specs=(vmem,) * 7,
         scratch_shapes=[
+            pltpu.VMEM((depth,) + panel.shape, F32),
             pltpu.VMEM((tp, total + blocks, SUB, BW), F32),
             pltpu.VMEM((n, tp, blocks, SUB, BW), F32),
             pltpu.VMEM((tt, n, blocks, SUB, BW), F32),
@@ -700,7 +777,9 @@
             dma((1 + tt,)),
         ]
         + [pltpu.VMEM((total + blocks, SUB, BW), F32)] * tt,
-        compiler_params=pltpu.CompilerParams(collective_id=3, has_side_effects=True),
+        compiler_params=pltpu.CompilerParams(
+            collective_id=3, has_side_effects=True, vmem_limit_bytes=40 << 20
+        ),
         cost_estimate=pl.CostEstimate(
             flops=0, bytes_accessed=40 * trail.size * 4, transcendentals=0
         ),
@@ -708,67 +787,96 @@
 
 
 def final_kernel(
-    root, full, reg, upper, inv, own, cross, r_ref, coupling_ref, q_ref, out_ref, weights
+    root,
+    early,
+    upper,
+    inv,
+    cross,
+    q,
+    reg,
+    high_ref,
+    low_ref,
+    r_ref,
+    coupling_ref,
+    q_ref,
+    out_ref,
+    late,
+    coupling,
+    sems,
 ):
     size = inv.shape[0]
-    ot, tt = reg.shape[0], reg.shape[1]
-    part = full.shape[2]
-
-    @pl.when(pl.program_id(0) == 0)
-    def _():
-        r_ref[...] = upper[...]
-        for t in range(tt):
-            rows = cross[t].reshape(ot * SUB, size)
-            turned = rows_dot(rows, inv[...], HIGHEST)
-            coupling_ref[:, t] = (turned * (1.0 / root)).reshape(ot, SUB, size)
-            weights[:, t] = plain_dot(turned, inv[...], HIGHEST).reshape(ot, SUB, size)
-
-    block = jnp.concatenate(
-        [full[:, :, k].reshape(size, BW) for k in range(part)], axis=1
+    ot, tt, blocks = reg.shape[:3]
+    rows_t = ot * SUB
+    chunks = list(range(early, tt))
+    steps = 2 if blocks % 2 == 0 else 1
+    span = blocks // steps
+    copies = [pltpu.make_async_copy(q, q_ref, sems.at[0])]
+    copies.append(pltpu.make_async_copy(upper, r_ref, sems.at[1]))
+    for t in range(early):
+        copies.append(pltpu.make_async_copy(reg.at[:, t], out_ref.at[:, t], sems.at[2 + t]))
+    for copy in copies:
+        copy.start()
+    rows = joined([cross[t].reshape(rows_t, size) for t in chunks])
+    left_side = three_part(rows_dot(rows, inv[...], HIGHEST))
+    narrow = min(4, span)
+    for h in range(steps):
+
+        def body(b, carry, h=h):
+            first = h * span + narrow * b
+            both = removed(left_side, high_ref, low_ref, first, narrow)
+            for k in range(narrow):
+                lanes = slice(k * BW, (k + 1) * BW)
+                for i, t in enumerate(chunks):
+                    part = both[i * rows_t : (i + 1) * rows_t, lanes]
+                    late[:, i, first + k] = reg[:, t, first + k] - part.reshape(ot, SUB, BW)
+            return carry
+
+        lax.fori_loop(0, span // narrow, body, 0)
+        for i, t in enumerate(chunks):
+            place = pl.ds(h * span, span)
+            copy = pltpu.make_async_copy(
+                late.at[:, i, place], out_ref.at[:, t, place], sems.at[2 + early + h * len(chunks) + i]
+            )
+            copy.start()
+            copies.append(copy)
+    every = jnp.stack([cross[t].reshape(ot, SUB, size) for t in range(tt)], axis=1)
+    coupling[...] = rows_dot(
+        inv[...] * (1.0 / root), every.reshape(ot * tt * SUB, size), HIGHEST
     )
-    both = plain_dot(weights[...].reshape(ot * tt * SUB, size), block, HIGH)
-    basis = plain_dot(own[...] * root, block, HIGH)
-    for k in range(part):
-        lanes = slice(k * BW, (k + 1) * BW)
-        out_ref[:, :, k] = reg[:, :, k] - both[:, lanes].reshape(ot, tt, SUB, BW)
-        q_ref[:, k] = basis[:, lanes].reshape(q_ref.shape[0], SUB, BW)
-
-
-def final(full, reg, upper, inv, own, cross, root):
-    depth, ctp, blocks = full.shape[:3]
+    last = pltpu.make_async_copy(coupling, coupling_ref, sems.at[2 + early + steps * len(chunks)])
+    last.start()
+    copies.append(last)
+    for copy in copies:
+        copy.wait()
+
+
+def final(upper, inv, cross, q, reg, high, low, root):
+    size = inv.shape[0]
     ot, tt = reg.shape[:2]
-    size = inv.shape[0]
-    part = 4 if blocks % 4 == 0 else 1
-    whole = lambda shape: pl.BlockSpec(shape, lambda i: (0,) * len(shape))
-    reg_spec = pl.BlockSpec((ot, tt, part, SUB, BW), lambda i: (0, 0, i, 0, 0))
+    early = min(2, tt - 1)
+    vmem = pl.BlockSpec(memory_space=pltpu.VMEM)
+    hbm = pl.BlockSpec(memory_space=pl.ANY)
+    near = [pltpu.with_memory_space_constraint(x, pltpu.VMEM) for x in (upper, inv, cross, q, reg, high, low)]
     return pl.pallas_call(
-        functools.partial(final_kernel, root),
-        grid=(blocks // part,),
+        functools.partial(final_kernel, root, early),
         out_shape=(
             jax.ShapeDtypeStruct((size, size), F32),
-            jax.ShapeDtypeStruct((ot, tt, SUB, size), F32),
-            jax.ShapeDtypeStruct((ctp, blocks, SUB, BW), F32),
-            jax.ShapeDtypeStruct((ot, tt, blocks, SUB, BW), F32),
+            jax.ShapeDtypeStruct((size, ot * tt * SUB), F32),
+            jax.ShapeDtypeStruct(q.shape, F32),
+            jax.ShapeDtypeStruct(reg.shape, F32),
         ),
-        in_specs=[
-            pl.BlockSpec((depth, ctp, part, SUB, BW), lambda i: (0, 0, i, 0, 0)),
-            reg_spec,
-            whole((size, size)),
-            whole((size, size)),
-            whole((size // depth, size)),
-            whole(cross.shape),
+        in_specs=[vmem] * 7,
+        out_specs=(hbm,) * 4,
+        scratch_shapes=[
+            pltpu.VMEM((ot, tt - early) + reg.shape[2:], F32),
+            pltpu.VMEM((size, ot * tt * SUB), F32),
+            pltpu.SemaphoreType.DMA((3 + early + 2 * (tt - early),)),
         ],
-        out_specs=(
-            whole((size, size)),
-            whole((ot, tt, SUB, size)),
-            pl.BlockSpec((ctp, part, SUB, BW), lambda i: (0, i, 0, 0)),
-            reg_spec,
+        compiler_params=pltpu.CompilerParams(vmem_limit_bytes=24 << 20),
+        cost_estimate=pl.CostEstimate(
+            flops=2 * size * reg.size, bytes_accessed=8 * reg.size, transcendentals=0
         ),
-        scratch_shapes=[pltpu.VMEM((ot, tt, SUB, size), F32)],
-        cost_estimate=pl.CostEstimate(
-            flops=2 * size * (reg.size + full.size), bytes_accessed=12 * reg.size, transcendentals=0
-        ),
-    )(full, reg, upper, inv, own, cross)
+    )(*near)
 
 
 def tiled(raw):
@@ -786,13 +894,14 @@
     depth = lax.axis_size("cols")
     pixels = raw_panel.shape[1]
     root = math.sqrt(pixels * n)
-    full, reg, upper, inv, own, cross = fused(
-        tiled(raw_panel), tiled(raw_trail), panel_shift, trail_shift, n, depth, 1.0 / root
+    raw = [
+        pltpu.with_memory_space_constraint(tiled(x), pltpu.HBM) for x in (raw_panel, raw_trail)
+    ]
+    held = fused(
+        *raw, panel_shift, trail_shift, n, depth, root
     )
-    r_factor, coupling, q_panel, out = final(full, reg, upper, inv, own, cross, root)
-    coupling = coupling.reshape(-1, coupling.shape[-1]).T
-    out = flat(out.reshape((-1,) + out.shape[2:]))
-    return (r_factor, coupling, flat(q_panel), out)
+    r_factor, coupling, q_panel, out = final(*held, root)
+    return (r_factor, coupling, flat(q_panel), flat(out.reshape((-1,) + out.shape[2:])))
 
 
 def solution(mesh):

time: 174 us -> 149 us (0.86)
  Pallas kernels: 172 us -> 146 us
    pallas_call x2, Pallas kernels: 172 us -> 146 us  [the longest x1 142 us: fused(): pl.pallas_call(functools.partial(fused_kernel, n, depth, pieces, root), o...]
    reshape x1 -> x0, local copies, waits for them, and re-layouts: 1.79 us -> none  [on_device(): coupling = coupling.reshape(-1, coupling.shape[-1]).T]
where the time goes in v2:
time: 149 us
  Pallas kernels  146 us (98%)
    pallas_call x1, Pallas kernels, fused(): pl.pallas_call(functools.partial(fused_kernel, n, depth, pieces, root), o...  142 us
    pallas_call x1, Pallas kernels, final(): pl.pallas_call(functools.partial(final_kernel, root, early), out_shape=(j...  3.9 us

profile of v2, /device:TPU:9, one launch (start us, length us, event | category | flops | bytes accessed | tf_op | source)
XLA Modules:
  0.0 148.5 jit_solution(15798657720827739449)
XLA Ops:
  0.6 0.0 copy-start
  0.6 0.7 copy-done
  1.3 0.0 copy-start.1
  1.3 0.7 copy-done.1
  2.0 142.5 %shard_map.75 = (f32[256,256]{1,0:T(8,128)S(1)}, f32[256,256]{1,0:T(8,128)S(1)}, f32[4,8,8,256]{3,2,1,0:T(8,128)S(1)}, f32[8,32,8,128]{3,2,1,0:T(8,128)S(1)}, f3...) custom-call(s32[64]{0:T(128)S(1)} %copy-done.1, ...), custom_call_target="tpu_custom_call" | custom-call | bytes 167772160 | tf_op jit(solution)/shard_map/pallas_call | solution.py:736
  144.5 3.9 %shard_map.76 = (f32[256,256]{1,0:T(8,128)}, f32[256,256]{1,0:T(8,128)}, f32[8,32,8,128]{3,2,1,0:T(8,128)}, f32[8,4,32,8,128]{4,3,2,1,0:T(8,128)}) custom-call(f32[256,256]{1,0:T(8,128)S(1)} %get-tuple-element.15.upper, f32[256,256]{1,0:T(8,128)S(1)} %get-tuple-element.16.inv, f32[4,8,8,256]{3,2,1,0:T(8,128)S(1)} %get-tuple-element.17.cross, ...), custom_call_target="tpu_custom_call" | custom-call | flops 536870912 | bytes 8388608 | tf_op jit(solution)/shard_map/pallas_call | solution.py:860
Async XLA Ops:
  0.6 0.7 copy-start
  1.3 0.7 copy-start.1

commit v3 on v2

--- a/solution.py
+++ b/solution.py
@@ -78,9 +78,12 @@
     ring_p,
     moved_p,
     moved_t,
-    gram_part,
-    gram_land,
-    gram_sum,
+    near_part,
+    near_land,
+    near_sum,
+    far_part,
+    far_land,
+    far_sum,
     cross_part,
     cross_land,
     aug,
@@ -116,8 +119,12 @@
     sr = cross_land.shape[2]
     oc = rows_t // sr
     size = inv_ref.shape[0]
-    mid_lo = max(depth // 2 - 1, 0)
-    mid_hi = min(depth // 2, depth - 1)
+    lead_z = max(depth // 2 - 1, 0)
+    leads = z == lead_z
+    tile = pair.shape[0]
+    tiles = size // tile
+    edge = size - tile
+    near_count = edge // (ctp * SUB)
     mine = pl.ds(pl.multiple_of(me * blocks, blocks), blocks)
 
     def each_peer(fn):
@@ -129,9 +136,7 @@
 
     def linked(other):
         near = (z - other == 1) | (other - z == 1)
-        low = ((z == mid_lo) & (other < mid_lo)) | ((z < mid_lo) & (other == mid_lo))
-        high = ((z == mid_hi) & (other > mid_hi)) | ((z > mid_hi) & (other == mid_hi))
-        return near | low | high
+        return near | (z != other) & (leads | (other == lead_z))
 
     barrier = pltpu.get_barrier_semaphore()
     for d in range(1, n):
@@ -162,8 +167,8 @@
         return row_copy(
             panel.at[pl.ds(to * tp, tp)],
             ring_p.at[:, mine],
-            p1_send.at[d - 1],
-            p1_recv.at[d - 1],
+            p1_send.at[0],
+            p1_recv.at[0],
             to,
         )
 
@@ -171,8 +176,8 @@
         return row_copy(
             moved_p.at[to],
             full.at[z, pl.ds(me * tp, tp)],
-            p2_send.at[d - 1],
-            p2_recv.at[d - 1],
+            p2_send.at[0],
+            p2_recv.at[0],
             to,
         )
 
@@ -180,8 +185,8 @@
         return row_copy(
             trail.at[to * tt + t],
             rings[t].at[mine],
-            t1_send.at[t, d - 1],
-            t1_recv.at[t, d - 1],
+            t1_send.at[t],
+            t1_recv.at[t],
             to,
         )
 
@@ -189,8 +194,8 @@
         return row_copy(
             moved_t.at[t, to],
             reg.at[me, t],
-            t2_send.at[t, d - 1],
-            t2_recv.at[t, d - 1],
+            t2_send.at[t],
+            t2_recv.at[t],
             to,
         )
 
@@ -203,29 +208,45 @@
             trail.at[me * tt + t], rings[t].at[mine], local_sem.at[1 + t]
         )
 
-    def started(copies, active, count):
-        def go(d, to, origin):
+    def started(copies, active, count, first=1, stride=1):
+        def go(k, carry):
+            d = first + stride * k
+            to = lax.rem(me + d, n)
+
             @only(active(to), count == n)
             def _():
                 copies(d, to).start()
 
-        each_peer(go)
-
-    def landed(copies, active, count, by_origin):
-        def go(d, to, origin):
-            @only(active(origin if by_origin else me), count == n)
+            return carry
+
+        lax.fori_loop(0, -(-(n - first) // stride), go, 0)
+
+    def whole(region, send, recv):
+        return row_copy(region, region, send, recv, lax.rem(me + 1, n))
+
+    def counted(active, count, per_copy, done):
+        if count == n:
+            done(per_copy(n - 1))
+        else:
+
+            @pl.when(active(me))
             def _():
-                copies(d, to).wait_recv()
-
-        each_peer(go)
-
-    def left(copies, active, count, by_target):
-        def go(d, to, origin):
-            @only(active(to if by_target else me), count == n)
+                done(per_copy(count - 1))
+
+            @pl.when(jnp.logical_not(active(me)))
             def _():
-                copies(d, to).wait_send()
-
-        each_peer(go)
+                done(per_copy(count))
+
+    def once(active, count, per_copy, done):
+        @only(active(me), count == n)
+        def _():
+            done(per_copy(n - 1))
+
+    def take(copy):
+        copy.wait_recv()
+
+    def clear(copy):
+        copy.wait_send()
 
     def has_p(j):
         return j < op
@@ -281,8 +302,8 @@
             device_id_type=MESH,
         )
 
-    def forward(d):
-        for q in range(pieces):
+    def forward(d, some=None):
+        for q in range(pieces) if some is None else some:
             for side in (0, 1):
 
                 @pl.when(receives(side, d))
@@ -295,19 +316,24 @@
                     def _():
                         line(side, d + 1, q).start()
 
-    def start_t1(t):
-        @only(has_t(me), ot == n)
-        def _():
-            own_t(t).start()
-
-        started(functools.partial(t1, t), has_t, ot)
+    def start_t1(t, halves=(0, 1)):
+        if 0 in halves:
+
+            @only(has_t(me), ot == n)
+            def _():
+                own_t(t).start()
+
+        if len(halves) == 2:
+            started(functools.partial(t1, t), has_t, ot)
+        else:
+            started(functools.partial(t1, t), has_t, ot, 2 - halves[0], 2)
 
     def turn_t(t):
         @only(has_t(me), ot == n)
         def _():
             own_t(t).wait()
 
-        landed(functools.partial(t1, t), has_t, ot, False)
+        once(has_t, ot, lambda k: whole(rings[t].at[pl.ds(0, k * blocks)], t1_send.at[t], t1_recv.at[t]), take)
 
         @only(has_t(me), ot == n)
         def _():
@@ -327,46 +353,84 @@
 
             compose(rings[t], shifts, me, keep)
 
-    def start_t2(t):
-        def go(d, to, origin):
-            t2(t, d, to).start()
-
+    def start_t2(t, halves=(0, 1)):
         @only(has_t(me), ot == n)
         def _():
-            each_peer(go)
+            if len(halves) == 2:
+                started(functools.partial(t2, t), has_t, n)
+            else:
+                started(functools.partial(t2, t), has_t, n, 2 - halves[0], 2)
 
     def wait_t2(t):
-        landed(functools.partial(t2, t), has_t, ot, True)
-
-    def panel_block(b, count):
-        cut = [full[:, :, count * b + k].reshape(size, BW) for k in range(count)]
+        counted(has_t, ot, lambda k: whole(reg.at[pl.ds(0, k), t], t2_send.at[t], t2_recv.at[t]), take)
+
+    def panel_block(b, count, lo=0, hi=depth):
+        rows = (hi - lo) * ctp * SUB
+        cut = [full[lo:hi, :, count * b + k].reshape(rows, BW) for k in range(count)]
         return jnp.concatenate(cut, axis=1)
 
     narrow = min(4, blocks)
     wide = min(8, blocks)
 
-    def make_gram():
-        gram_part[...] = jnp.zeros_like(gram_part)
+    def gram_near():
+        near_part[...] = jnp.zeros_like(near_part)
 
         def body(b, carry):
-            block = panel_block(b, narrow)
-            gram_part[...] += rows_dot(block, block, HIGHEST).reshape(gram_part.shape)
+            block = panel_block(b, narrow, 0, near_count)
+            near_part[...] += rows_dot(block, block, HIGHEST).reshape(near_part.shape)
             return carry
 
         lax.fori_loop(0, blocks // narrow, body, 0)
 
-    def g_one(d, to):
-        return row_copy(
-            gram_part.at[to], gram_land.at[d - 1], g_send.at[0, d - 1], g_recv.at[0, d - 1], to
-        )
-
-    def g_two(d, to):
-        return row_copy(
-            gram_sum.at[me], gram_sum.at[me], g_send.at[1, d - 1], g_recv.at[1, d - 1], to
-        )
-
-    def every(j):
-        return j >= 0
+    def gram_far():
+        far_part[...] = jnp.zeros_like(far_part)
+
+        def body(b, carry):
+            block = panel_block(b, narrow, near_count, depth)
+            both = rows_dot(block, panel_block(b, narrow), HIGHEST)
+            far_part[...] += both.reshape(far_part.shape)
+            return carry
+
+        lax.fori_loop(0, blocks // narrow, body, 0)
+
+    grams = ((near_part, near_land, near_sum), (far_part, far_land, far_sum))
+
+    def g_one(k, d, to):
+        part, land, _ = grams[k]
+        return row_copy(part.at[to], land.at[d - 1], g_send.at[k, 0], g_recv.at[k, 0], to)
+
+    def g_two(k, d, to):
+        ref = grams[k][2]
+        return row_copy(ref.at[me], ref.at[me], g_send.at[k, 1], g_recv.at[k, 1], to)
+
+    def g_count(k):
+        return grams[k][0].shape[0]
+
+    def has_g(k):
+        return lambda j: j < g_count(k)
+
+    def gram_scatter(k):
+        started(functools.partial(g_one, k), has_g(k), g_count(k))
+
+    def gram_spread(k):
+        part, land, total_ref = grams[k]
+
+        @only(me < g_count(k), g_count(k) == n)
+        def _():
+            take(whole(land, g_send.at[k, 0], g_recv.at[k, 0]))
+            total_g = part[me]
+            for d in range(1, n):
+                total_g = total_g + land[d - 1]
+            total_ref[me] = total_g
+
+            def go(d, to, origin):
+                g_two(k, d, to).start()
+
+            each_peer(go)
+
+    def gram_done(k):
+        ref = grams[k][2]
+        counted(has_g(k), g_count(k), lambda m: whole(ref.at[pl.ds(0, m)], g_send.at[k, 1], g_recv.at[k, 1]), take)
 
     def has_c(j):
         return j < oc
@@ -387,8 +451,8 @@
         return row_copy(
             cross_part.at[t, to],
             cross_land.at[t, d - 1],
-            c_send.at[0, t, d - 1],
-            c_recv.at[0, t, d - 1],
+            c_send.at[0, t],
+            c_recv.at[0, t],
             to,
         )
 
@@ -396,8 +460,8 @@
         return row_copy(
             cross_ref.at[t, me],
             cross_ref.at[t, me],
-            c_send.at[1, t, d - 1],
-            c_recv.at[1, t, d - 1],
+            c_send.at[1, t],
+            c_recv.at[1, t],
             to,
         )
 
@@ -407,9 +471,9 @@
     def cross_spread(t):
         @only(has_c(me), oc == n)
         def _():
+            take(whole(cross_land.at[t], c_send.at[0, t], c_recv.at[0, t]))
             total_c = cross_part[t, me]
             for d in range(1, n):
-                c_one(t, d, lax.rem(me + d, n)).wait_recv()
                 total_c = total_c + cross_land[t, d - 1]
             cross_ref[t, me] = total_c
 
@@ -419,12 +483,7 @@
             each_peer(go)
 
     def cross_done(t):
-        landed(functools.partial(c_two, t), has_c, oc, True)
-
-    tile = min(64, size)
-    tiles = size // tile
-    low_count = mid_lo
-    high_count = depth - 1 - mid_hi
+        counted(has_c, oc, lambda k: whole(cross_ref.at[t, pl.ds(0, k)], c_send.at[1, t], c_recv.at[1, t]), take)
 
     def factor_copy(i, k, slot, to):
         ref = inv_ref if k == 0 else upper_ref
@@ -432,29 +491,27 @@
         return pltpu.make_async_remote_copy(
             src_ref=ref.at[rows],
             dst_ref=ref.at[rows],
-            send_sem=f_send.at[slot, i, k],
-            recv_sem=f_recv.at[i, k],
+            send_sem=f_send.at[slot, k],
+            recv_sem=f_recv.at[k],
             device_id={"cols": to},
             device_id_type=MESH,
         )
 
-    def factor_sends(act):
-        for k in (0, 1):
-            for i in range(tiles):
-                send_factor(i, k, act)
+    def factor_whole(k, slot=0):
+        ref = inv_ref if k == 0 else upper_ref
+        return pltpu.make_async_remote_copy(
+            src_ref=ref,
+            dst_ref=ref,
+            send_sem=f_send.at[slot, k],
+            recv_sem=f_recv.at[k],
+            device_id={"cols": lax.rem(z + 1, depth)},
+            device_id_type=MESH,
+        )
 
     def send_factor(i, k, act):
-        for slot in range(low_count):
-
-            @pl.when(z == mid_lo)
-            def _():
-                act(factor_copy(i, k, slot, slot))
-
-        for slot in range(high_count):
-
-            @pl.when(z == mid_hi)
-            def _():
-                act(factor_copy(i, k, slot, mid_hi + 1 + slot))
+        for other in range(depth):
+            if other != lead_z:
+                act(factor_copy(i, k, other, other))
 
     def factor_tile(i):
         lo = i * tile
@@ -484,7 +541,7 @@
         upper = jnp.where(gcol >= grow, lead_rows[:, 0:size], 0.0)
         upper_ref[lo:hi, :] = upper * (1.0 / root)
         inv_ref[lo:hi, :] = lead_rows[:, size : 2 * size]
-        if hi < size:
+        if hi < edge:
             aug[...] = aug[...] - lax.dot_general(
                 upper,
                 lead_rows,
@@ -543,7 +600,7 @@
     def _():
         own_p.wait()
 
-    landed(p1, has_p, op, False)
+    once(has_p, op, lambda k: whole(ring_p.at[:, pl.ds(0, k * blocks)], p1_send.at[0], p1_recv.at[0]), take)
 
     @only(has_p(me), op == n)
     def _():
@@ -578,7 +635,7 @@
     start_t1(0)
     if tt > 1:
         start_t1(1)
-    landed(p2, has_p, op, True)
+    counted(has_p, op, lambda k: whole(full.at[z, pl.ds(0, k * tp)], p2_send.at[0], p2_recv.at[0]), take)
     for q in range(pieces):
         for side in (0, 1):
 
@@ -590,36 +647,29 @@
     turn_t(0)
     if last > 0:
         start_t2(0)
-    for t in range(2, last):
-        start_t1(t)
-    if depth > 1:
-        forward(1)
-    for t in range(1, last):
-        turn_t(t)
-        if t + 1 < last:
-            start_t2(t)
-        if t == 1:
-            for d in range(2, middle + 1):
-                forward(d)
-    if last < 2:
-        for d in range(2, middle + 1):
-            forward(d)
+    follows = jnp.logical_not(leads)
+
+    @pl.when(follows)
+    def _():
+        for t in range(2, last):
+            start_t1(t)
+
+    for d in range(1, middle):
+        forward(d)
 
     def rest_t1():
         if last > 1:
             start_t1(last)
 
     def rest_t2():
-        if last > 1:
-            start_t2(last - 1)
+        for t in range(2, last):
+            start_t2(t)
 
     def finish_turns():
         if last > 0:
             turn_t(last)
         start_t2(last)
 
-    central = (z == mid_lo) | (z == mid_hi)
-
     def cross_chunk(t):
         wait_t2(t)
         make_cross(t)
@@ -627,84 +677,127 @@
 
     early = min(2, last)
 
-    @pl.when(central)
+    def border():
+        far = far_sum[...].reshape(tile, size)
+        corner = rows_dot(inv_ref[0:edge, 0:edge], far[:, 0:edge], HIGHEST)
+        upper_ref[0:edge, edge:size] = corner * (1.0 / root)
+
+        def turned(right):
+            return lax.dot_general(
+                corner,
+                right,
+                (((0,), (0,)), ((), ())),
+                precision=HIGHEST,
+                preferred_element_type=F32,
+            )
+
+        aug[edge:size, edge:size] = far[:, edge:size] - turned(corner)
+        aug[edge:size, size : 2 * size] = aug[edge:size, size : 2 * size] - turned(inv_ref[0:edge, :])
+
+    @pl.when(leads)
     def _():
-        make_gram()
-        started(g_one, every, n)
-        aug_row = lax.broadcasted_iota(jnp.int32, (size, size), 0)
-        aug_col = lax.broadcasted_iota(jnp.int32, (size, size), 1)
-        aug[:, size : 2 * size] = jnp.where(aug_row == aug_col, 1.0, 0.0)
-        if early > 0:
-            cross_chunk(0)
-        total_g = gram_part[me]
-        for d in range(1, n):
-            g_one(d, lax.rem(me + d, n)).wait_recv()
-            total_g = total_g + gram_land[d - 1]
-        gram_sum[me] = total_g
-        started(g_two, every, n)
-        rest_t1()
-        rest_t2()
-        if early > 1:
-            cross_chunk(1)
-        landed(g_two, every, n, True)
-        aug[:, 0:size] = gram_sum[...].reshape(size, size)
-        for i in range(tiles):
+        gram_near()
+        gram_scatter(0)
+        if last > 2:
+            start_t1(2, (0,))
+        if last > 1:
+            turn_t(1)
+        aug_row = lax.broadcasted_iota(jnp.int32, (size, 2 * size), 0)
+        aug_col = lax.broadcasted_iota(jnp.int32, (size, 2 * size), 1)
+        aug[...] = jnp.where(aug_col == aug_row + size, 1.0, 0.0)
+        gram_spread(0)
+        for t in range(2, last):
+            start_t1(t, (1,) if t == 2 else (0, 1))
+        if last > 1:
+            start_t2(1)
+        forward(middle, range(pieces // 2))
+        gram_done(0)
+        forward(middle, range(pieces // 2, pieces - 1))
+        aug[0:edge, 0:edge] = near_sum[...].reshape(edge, edge)
+        for i in range(tiles - 1):
             factor_tile(i)
             send_factor(i, 0, start_copy)
-            if i == min(1, tiles - 1):
-                finish_turns()
+            if i == 0:
+                forward(middle, range(pieces - 1, pieces))
+                gram_far()
+                gram_scatter(1)
+                if last > 1:
+                    start_t1(last, (0,))
+                for t in range(2, last):
+                    turn_t(t)
+            if i == min(1, tiles - 2):
+                gram_spread(1)
+                if last > 1:
+                    start_t1(last, (1,))
+                rest_t2()
+        gram_done(1)
+        border()
+        factor_tile(tiles - 1)
+        send_factor(tiles - 1, 0, start_copy)
         for i in range(tiles):
             send_factor(i, 1, start_copy)
         for t in range(early):
-            cross_spread(t)
-        for t in range(early, last):
             cross_chunk(t)
-        left(g_one, every, n, True)
-        left(g_two, every, n, True)
-
-    @pl.when(jnp.logical_not(central))
+        finish_turns()
+        for k in (0, 1):
+            part, land, _ = grams[k]
+            row = lambda m: pl.ds(0, m)
+            counted(has_g(k), g_count(k), lambda m: whole(land.at[row(m)], g_send.at[k, 0], g_recv.at[k, 0]), clear)
+            once(has_g(k), g_count(k), lambda m: whole(land.at[row(m)], g_send.at[k, 1], g_recv.at[k, 1]), clear)
+
+    @pl.when(follows)
     def _():
+        for t in range(1, last):
+            turn_t(t)
+            if t == 1:
+                start_t2(t)
+                for d in range(middle, middle + 1):
+                    forward(d)
+        if last < 2:
+            for d in range(middle, middle + 1):
+                forward(d)
         rest_t1()
         rest_t2()
+        finish_turns()
         for d in range(middle + 1, depth):
             forward(d)
-        finish_turns()
-        for t in range(last):
+        for t in range(early):
             cross_chunk(t)
-        for t in range(early):
-            cross_spread(t)
-
+        factor_whole(0).wait_recv()
+
+    make_basis()
+    for t in range(early, last):
+        cross_chunk(t)
+    for t in range(early):
+        cross_spread(t)
     cross_chunk(last)
-
-    @pl.when(jnp.logical_not(central))
+    for t in range(early, last):
+        cross_spread(t)
+    cross_spread(last)
+    if last > 0:
+        emit(list(range(last)))
+    cross_done(last)
+
+    @pl.when(follows)
     def _():
-        for i in range(tiles):
-            factor_copy(i, 0, 0, mid_lo).wait_recv()
-
-    make_basis()
-    for t in range(early, tt):
-        cross_spread(t)
-    if early > 0:
-        emit(list(range(early)))
-    for t in range(early, tt):
-        cross_done(t)
-
-    @pl.when(jnp.logical_not(central))
+        factor_whole(1).wait_recv()
+
+    @pl.when(leads)
     def _():
-        for i in range(tiles):
-            factor_copy(i, 1, 0, mid_lo).wait_recv()
-
-    @pl.when(central)
-    def _():
-        factor_sends(lambda copy: copy.wait_send())
-
-    left(p1, has_p, op, True)
-    left(p2, has_p, op, False)
+        for other in range(depth):
+            if other != lead_z:
+                for k in (0, 1):
+                    factor_whole(k, other).wait_send()
+
+    counted(has_p, op, lambda k: whole(ring_p.at[:, pl.ds(0, k * blocks)], p1_send.at[0], p1_recv.at[0]), clear)
+    once(has_p, op, lambda k: whole(ring_p.at[:, pl.ds(0, k * blocks)], p2_send.at[0], p2_recv.at[0]), clear)
     for t in range(tt):
-        left(functools.partial(t1, t), has_t, ot, True)
-        left(functools.partial(t2, t), has_t, ot, False)
-        left(functools.partial(c_one, t), has_c, oc, True)
-        left(functools.partial(c_two, t), has_c, oc, False)
+        ring = rings[t]
+        counted(has_t, ot, lambda k: whole(ring.at[pl.ds(0, k * blocks)], t1_send.at[t], t1_recv.at[t]), clear)
+        once(has_t, ot, lambda k: whole(ring.at[pl.ds(0, k * blocks)], t2_send.at[t], t2_recv.at[t]), clear)
+        land = cross_land.at[t]
+        counted(has_c, oc, lambda k: whole(land.at[pl.ds(0, k)], c_send.at[0, t], c_recv.at[0, t]), clear)
+        once(has_c, oc, lambda k: whole(land.at[pl.ds(0, k)], c_send.at[1, t], c_recv.at[1, t]), clear)
     for d in range(1, depth):
         for q in range(pieces):
             for side in (0, 1):
@@ -724,7 +817,11 @@
     rows_t = ot * SUB
     sr = max(SUB, rows_t // n)
     oc = rows_t // sr
-    tiles = max(size // 64, 1)
+    tile = 64
+    tiles = size // tile
+    edge = size - tile
+    near_rows = -(-edge // (n * SUB)) * SUB
+    far_rows = -(-tile // (n * SUB)) * SUB
     pieces = 4 if ctp % 4 == 0 else 1
     total = n * blocks
     smem = pl.BlockSpec(memory_space=pltpu.SMEM)
@@ -751,29 +848,32 @@
             pltpu.VMEM((tp, total + blocks, SUB, BW), F32),
             pltpu.VMEM((n, tp, blocks, SUB, BW), F32),
             pltpu.VMEM((tt, n, blocks, SUB, BW), F32),
-            pltpu.VMEM((n, size // n, size), F32),
-            pltpu.VMEM((peers, size // n, size), F32),
-            pltpu.VMEM((n, size // n, size), F32),
+            pltpu.VMEM((edge // near_rows, near_rows, edge), F32),
+            pltpu.VMEM((peers, near_rows, edge), F32),
+            pltpu.VMEM((edge // near_rows, near_rows, edge), F32),
+            pltpu.VMEM((tile // far_rows, far_rows, size), F32),
+            pltpu.VMEM((peers, far_rows, size), F32),
+            pltpu.VMEM((tile // far_rows, far_rows, size), F32),
             pltpu.VMEM((tt, oc, sr, size), F32),
             pltpu.VMEM((tt, peers, sr, size), F32),
             pltpu.VMEM((size, 2 * size), F32),
-            pltpu.VMEM((size // tiles, 2 * (size // tiles)), F32),
-            dma((peers,)),
-            dma((peers,)),
-            dma((peers,)),
-            dma((peers,)),
-            dma((tt, peers)),
-            dma((tt, peers)),
-            dma((tt, peers)),
-            dma((tt, peers)),
+            pltpu.VMEM((tile, 2 * tile), F32),
+            dma((1,)),
+            dma((1,)),
+            dma((1,)),
+            dma((1,)),
+            dma((tt,)),
+            dma((tt,)),
+            dma((tt,)),
+            dma((tt,)),
             dma((2, lines, pieces)),
             dma((2, lines, pieces)),
-            dma((2, peers)),
-            dma((2, peers)),
-            dma((2, tt, peers)),
-            dma((2, tt, peers)),
-            dma((lines, tiles, 2)),
-            dma((tiles, 2)),
+            dma((2, 2)),
+            dma((2, 2)),
+            dma((2, tt)),
+            dma((2, tt)),
+            dma((depth, 2)),
+            dma((2,)),
             dma((1 + tt,)),
         ]
         + [pltpu.VMEM((total + blocks, SUB, BW), F32)] * tt,
@@ -853,7 +953,7 @@
 def final(upper, inv, cross, q, reg, high, low, root):
     size = inv.shape[0]
     ot, tt = reg.shape[:2]
-    early = min(2, tt - 1)
+    early = tt - 1
     vmem = pl.BlockSpec(memory_space=pltpu.VMEM)
     hbm = pl.BlockSpec(memory_space=pl.ANY)
     near = [pltpu.with_memory_space_constraint(x, pltpu.VMEM) for x in (upper, inv, cross, q, reg, high, low)]

time: 149 us -> 144 us (0.966)
  Pallas kernels: 146 us -> 141 us
    pallas_call x1, Pallas kernels: 142 us -> 138 us  [fused(): pl.pallas_call(functools.partial(fused_kernel, n, depth, pieces, root), o...]
where the time goes in v3:
time: 144 us
  Pallas kernels  141 us (98%)
    pallas_call x1, Pallas kernels, fused(): pl.pallas_call(functools.partial(fused_kernel, n, depth, pieces, root), o...  138 us
    pallas_call x1, Pallas kernels, final(): pl.pallas_call(functools.partial(final_kernel, root, early), out_shape=(j...  3.69 us

profile of v3, /device:TPU:9, one launch (start us, length us, event | category | flops | bytes accessed | tf_op | source)
XLA Modules:
  0.0 143.5 jit_solution(2788257548352446038)
XLA Ops:
  0.6 0.0 copy-start
  0.6 0.7 copy-done
  1.3 0.0 copy-start.1
  1.3 0.7 copy-done.1
  2.0 137.7 %shard_map.75 = (f32[256,256]{1,0:T(8,128)S(1)}, f32[256,256]{1,0:T(8,128)S(1)}, f32[4,8,8,256]{3,2,1,0:T(8,128)S(1)}, f32[8,32,8,128]{3,2,1,0:T(8,128)S(1)}, f3...) custom-call(s32[64]{0:T(128)S(1)} %copy-done.1, ...), custom_call_target="tpu_custom_call" | custom-call | bytes 167772160 | tf_op jit(solution)/shard_map/pallas_call | solution.py:833
  139.7 3.7 %shard_map.76 = (f32[256,256]{1,0:T(8,128)}, f32[256,256]{1,0:T(8,128)}, f32[8,32,8,128]{3,2,1,0:T(8,128)}, f32[8,4,32,8,128]{4,3,2,1,0:T(8,128)}) custom-call(f32[256,256]{1,0:T(8,128)S(1)} %get-tuple-element.15.upper, f32[256,256]{1,0:T(8,128)S(1)} %get-tuple-element.16.inv, f32[4,8,8,256]{3,2,1,0:T(8,128)S(1)} %get-tuple-element.17.cross, ...), custom_call_target="tpu_custom_call" | custom-call | flops 536870912 | bytes 8388608 | tf_op jit(solution)/shard_map/pallas_call | solution.py:960
Async XLA Ops:
  0.6 0.7 copy-start
  1.3 0.7 copy-start.1

commit v4 on v3

--- a/solution.py
+++ b/solution.py
@@ -78,6 +78,7 @@
     ring_p,
     moved_p,
     moved_t,
+    near_all,
     near_part,
     near_land,
     near_sum,
@@ -190,12 +191,13 @@
             to,
         )
 
-    def t2(t, d, to):
+    def t2(t, half, d, to):
+        cut = pl.ds(0, blocks) if half is None else pl.ds(half * (blocks // 2), blocks // 2)
         return row_copy(
-            moved_t.at[t, to],
-            reg.at[me, t],
-            t2_send.at[t],
-            t2_recv.at[t],
+            moved_t.at[t, to, cut],
+            reg.at[me, t, cut],
+            t2_send.at[t + (1 if half == 1 else 0)],
+            t2_recv.at[t + (1 if half == 1 else 0)],
             to,
         )
 
@@ -208,12 +210,13 @@
             trail.at[me * tt + t], rings[t].at[mine], local_sem.at[1 + t]
         )
 
-    def started(copies, active, count, first=1, stride=1):
+    def started(copies, active, count, first=1, stride=1, pick=None):
         def go(k, carry):
             d = first + stride * k
             to = lax.rem(me + d, n)
-
-            @only(active(to), count == n)
+            wanted = active(to) if pick is None else active(to) & pick(d)
+
+            @only(wanted, count == n and pick is None)
             def _():
                 copies(d, to).start()
 
@@ -353,16 +356,16 @@
 
             compose(rings[t], shifts, me, keep)
 
-    def start_t2(t, halves=(0, 1)):
+    def start_t2(t):
         @only(has_t(me), ot == n)
         def _():
-            if len(halves) == 2:
-                started(functools.partial(t2, t), has_t, n)
-            else:
-                started(functools.partial(t2, t), has_t, n, 2 - halves[0], 2)
-
-    def wait_t2(t):
-        counted(has_t, ot, lambda k: whole(reg.at[pl.ds(0, k), t], t2_send.at[t], t2_recv.at[t]), take)
+            for half in (0, 1) if t == tt - 1 else (None,):
+                started(functools.partial(t2, t, half), has_t, n)
+
+    def wait_t2(t, half=None):
+        cut = pl.ds(0, blocks if half is None else blocks // 2)
+        sem = t + (1 if half == 1 else 0)
+        counted(has_t, ot, lambda k: whole(reg.at[pl.ds(0, k), t, cut], t2_send.at[sem], t2_recv.at[sem]), take)
 
     def panel_block(b, count, lo=0, hi=depth):
         rows = (hi - lo) * ctp * SUB
@@ -370,17 +373,26 @@
         return jnp.concatenate(cut, axis=1)
 
     narrow = min(4, blocks)
-    wide = min(8, blocks)
+    wide = min(8, blocks // 2)
 
     def gram_near():
-        near_part[...] = jnp.zeros_like(near_part)
+        near_all[...] = jnp.zeros_like(near_all)
 
         def body(b, carry):
             block = panel_block(b, narrow, 0, near_count)
-            near_part[...] += rows_dot(block, block, HIGHEST).reshape(near_part.shape)
+            near_all[...] += rows_dot(block, block, HIGHEST)
             return carry
 
         lax.fori_loop(0, blocks // narrow, body, 0)
+        packed = [near_all[lo : lo + tile, lo:edge] for lo in range(0, edge, tile)]
+        near_part[...] = jnp.concatenate(packed, axis=1).reshape(near_part.shape)
+
+    def unpack_near():
+        packed = near_sum[...].reshape(tile, near_sum.shape[2])
+        first = 0
+        for lo in range(0, edge, tile):
+            aug[lo : lo + tile, lo:edge] = packed[:, first : first + edge - lo]
+            first += edge - lo
 
     def gram_far():
         far_part[...] = jnp.zeros_like(far_part)
@@ -435,8 +447,9 @@
     def has_c(j):
         return j < oc
 
-    def make_cross(t):
-        cross_part[t] = jnp.zeros_like(cross_part[t])
+    def make_cross(t, lo=0, hi=blocks):
+        if lo == 0:
+            cross_part[t] = jnp.zeros_like(cross_part[t])
 
         def body(b, carry):
             cut = [reg[:, t, wide * b + k].reshape(rows_t, BW) for k in range(wide)]
@@ -445,7 +458,7 @@
             cross_part[t] += both.reshape(oc, sr, size)
             return carry
 
-        lax.fori_loop(0, blocks // wide, body, 0)
+        lax.fori_loop(lo // wide, hi // wide, body, 0)
 
     def c_one(t, d, to):
         return row_copy(
@@ -576,16 +589,16 @@
         left_side = three_part(rows_dot(joined(rows), inv_ref[...], HIGHEST))
 
         def body(b, carry):
-            both = removed(left_side, high_ref, low_ref, narrow * b, narrow)
-            for k in range(narrow):
+            both = removed(left_side, high_ref, low_ref, wide * b, wide)
+            for k in range(wide):
                 lanes = slice(k * BW, (k + 1) * BW)
-                place = narrow * b + k
+                place = wide * b + k
                 for i, t in enumerate(chunks):
                     part = both[i * rows_t : (i + 1) * rows_t, lanes]
                     reg[:, t, place] = reg[:, t, place] - part.reshape(ot, SUB, BW)
             return carry
 
-        lax.fori_loop(0, blocks // narrow, body, 0)
+        lax.fori_loop(0, blocks // wide, body, 0)
 
     def start_copy(copy):
         copy.start()
@@ -595,6 +608,15 @@
         own_p.start()
 
     started(p1, has_p, op)
+
+    def ahead(d):
+        return (d == 2) | (d == 4)
+
+    @only(has_t(me), ot == n)
+    def _():
+        own_t(0).start()
+
+    started(functools.partial(t1, 0), has_t, ot, pick=ahead)
 
     @only(has_p(me), op == n)
     def _():
@@ -632,7 +654,7 @@
             compose(ring_p.at[t], shifts[t], me, keep)
 
     last = tt - 1
-    start_t1(0)
+    started(functools.partial(t1, 0), has_t, ot, pick=lambda d: jnp.logical_not(ahead(d)))
     if tt > 1:
         start_t1(1)
     counted(has_p, op, lambda k: whole(full.at[z, pl.ds(0, k * tp)], p2_send.at[0], p2_recv.at[0]), take)
@@ -671,8 +693,14 @@
         start_t2(last)
 
     def cross_chunk(t):
-        wait_t2(t)
-        make_cross(t)
+        if t == last:
+            wait_t2(t, 0)
+            make_cross(t, 0, blocks // 2)
+            wait_t2(t, 1)
+            make_cross(t, blocks // 2, blocks)
+        else:
+            wait_t2(t)
+            make_cross(t)
         cross_scatter(t)
 
     early = min(2, last)
@@ -713,7 +741,7 @@
         forward(middle, range(pieces // 2))
         gram_done(0)
         forward(middle, range(pieces // 2, pieces - 1))
-        aug[0:edge, 0:edge] = near_sum[...].reshape(edge, edge)
+        unpack_near()
         for i in range(tiles - 1):
             factor_tile(i)
             send_factor(i, 0, start_copy)
@@ -736,9 +764,9 @@
         send_factor(tiles - 1, 0, start_copy)
         for i in range(tiles):
             send_factor(i, 1, start_copy)
+        finish_turns()
         for t in range(early):
             cross_chunk(t)
-        finish_turns()
         for k in (0, 1):
             part, land, _ = grams[k]
             row = lambda m: pl.ds(0, m)
@@ -768,10 +796,8 @@
     make_basis()
     for t in range(early, last):
         cross_chunk(t)
-    for t in range(early):
-        cross_spread(t)
     cross_chunk(last)
-    for t in range(early, last):
+    for t in range(last):
         cross_spread(t)
     cross_spread(last)
     if last > 0:
@@ -794,7 +820,9 @@
     for t in range(tt):
         ring = rings[t]
         counted(has_t, ot, lambda k: whole(ring.at[pl.ds(0, k * blocks)], t1_send.at[t], t1_recv.at[t]), clear)
-        once(has_t, ot, lambda k: whole(ring.at[pl.ds(0, k * blocks)], t2_send.at[t], t2_recv.at[t]), clear)
+        for sem in (t, t + 1) if t == tt - 1 else (t,):
+            bulk = blocks // 2 if t == tt - 1 else blocks
+            once(has_t, ot, lambda k: whole(ring.at[pl.ds(0, k * bulk)], t2_send.at[sem], t2_recv.at[sem]), clear)
         land = cross_land.at[t]
         counted(has_c, oc, lambda k: whole(land.at[pl.ds(0, k)], c_send.at[0, t], c_recv.at[0, t]), clear)
         once(has_c, oc, lambda k: whole(land.at[pl.ds(0, k)], c_send.at[1, t], c_recv.at[1, t]), clear)
@@ -820,7 +848,7 @@
     tile = 64
     tiles = size // tile
     edge = size - tile
-    near_rows = -(-edge // (n * SUB)) * SUB
+    packed = tile * (tiles * (tiles - 1) // 2)
     far_rows = -(-tile // (n * SUB)) * SUB
     pieces = 4 if ctp % 4 == 0 else 1
     total = n * blocks
@@ -848,9 +876,10 @@
             pltpu.VMEM((tp, total + blocks, SUB, BW), F32),
             pltpu.VMEM((n, tp, blocks, SUB, BW), F32),
             pltpu.VMEM((tt, n, blocks, SUB, BW), F32),
-            pltpu.VMEM((edge // near_rows, near_rows, edge), F32),
-            pltpu.VMEM((peers, near_rows, edge), F32),
-            pltpu.VMEM((edge // near_rows, near_rows, edge), F32),
+            pltpu.VMEM((edge, edge), F32),
+            pltpu.VMEM((tile // far_rows, far_rows, packed), F32),
+            pltpu.VMEM((peers, far_rows, packed), F32),
+            pltpu.VMEM((tile // far_rows, far_rows, packed), F32),
             pltpu.VMEM((tile // far_rows, far_rows, size), F32),
             pltpu.VMEM((peers, far_rows, size), F32),
             pltpu.VMEM((tile // far_rows, far_rows, size), F32),
@@ -864,8 +893,8 @@
             dma((1,)),
             dma((tt,)),
             dma((tt,)),
-            dma((tt,)),
-            dma((tt,)),
+            dma((tt + 1,)),
+            dma((tt + 1,)),
             dma((2, lines, pieces)),
             dma((2, lines, pieces)),
             dma((2, 2)),
@@ -918,7 +947,7 @@
         copy.start()
     rows = joined([cross[t].reshape(rows_t, size) for t in chunks])
     left_side = three_part(rows_dot(rows, inv[...], HIGHEST))
-    narrow = min(4, span)
+    narrow = min(8, span)
     for h in range(steps):
 
         def body(b, carry, h=h):
@@ -997,8 +1026,11 @@
     raw = [
         pltpu.with_memory_space_constraint(tiled(x), pltpu.HBM) for x in (raw_panel, raw_trail)
     ]
+    shifts = [
+        pltpu.with_memory_space_constraint(x, pltpu.HBM) for x in (panel_shift, trail_shift)
+    ]
     held = fused(
-        *raw, panel_shift, trail_shift, n, depth, root
+        *raw, *shifts, n, depth, root
     )
     r_factor, coupling, q_panel, out = final(*held, root)
     return (r_factor, coupling, flat(q_panel), flat(out.reshape((-1,) + out.shape[2:])))

time: 144 us -> 139 us (0.965)
  Pallas kernels: 141 us -> 138 us
    pallas_call x1, Pallas kernels: 138 us -> 135 us  [fused(): pl.pallas_call(functools.partial(fused_kernel, n, depth, pieces, root), o...]
where the time goes in v4:
time: 139 us
  Pallas kernels  138 us (99%)
    pallas_call x1, Pallas kernels, fused(): pl.pallas_call(functools.partial(fused_kernel, n, depth, pieces, root), o...  135 us
    pallas_call x1, Pallas kernels, final(): pl.pallas_call(functools.partial(final_kernel, root, early), out_shape=(j...  3.12 us

profile of v4, /device:TPU:9, one launch (start us, length us, event | category | flops | bytes accessed | tf_op | source)
XLA Modules:
  0.0 138.9 jit_solution(15492496637490185048)
XLA Ops:
  0.6 135.0 %shard_map.75 = (f32[256,256]{1,0:T(8,128)S(1)}, f32[256,256]{1,0:T(8,128)S(1)}, f32[4,8,8,256]{3,2,1,0:T(8,128)S(1)}, f32[8,32,8,128]{3,2,1,0:T(8,128)S(1)}, f3...) custom-call(s32[64]{0:T(128)} %panel_shift.1, ...), custom_call_target="tpu_custom_call" | custom-call | bytes 167772160 | tf_op jit(solution)/shard_map/pallas_call | solution.py:861
  135.7 3.1 %shard_map.76 = (f32[256,256]{1,0:T(8,128)}, f32[256,256]{1,0:T(8,128)}, f32[8,32,8,128]{3,2,1,0:T(8,128)}, f32[8,4,32,8,128]{4,3,2,1,0:T(8,128)}) custom-call(f32[256,256]{1,0:T(8,128)S(1)} %get-tuple-element.15.upper, f32[256,256]{1,0:T(8,128)S(1)} %get-tuple-element.16.inv, f32[4,8,8,256]{3,2,1,0:T(8,128)S(1)} %get-tuple-element.17.cross, ...), custom_call_target="tpu_custom_call" | custom-call | flops 536870912 | bytes 8388608 | tf_op jit(solution)/shard_map/pallas_call | solution.py:989

commit v5 on v4

--- a/solution.py
+++ b/solution.py
@@ -105,6 +105,8 @@
     c_recv,
     f_send,
     f_recv,
+    h_send,
+    h_recv,
     local_sem,
     *rings,
 ):
@@ -122,6 +124,8 @@
     size = inv_ref.shape[0]
     lead_z = max(depth // 2 - 1, 0)
     leads = z == lead_z
+    helper_z = min(lead_z + 1, depth - 1)
+    helps = z == helper_z
     tile = pair.shape[0]
     tiles = size // tile
     edge = size - tile
@@ -319,15 +323,21 @@
                     def _():
                         line(side, d + 1, q).start()
 
-    def start_t1(t, halves=(0, 1)):
-        if 0 in halves:
+    def ahead(d):
+        return (d == 2) | (d == 4)
+
+    def behind(d):
+        return jnp.logical_not(ahead(d))
+
+    def start_t1(t, halves=(0, 1), picked=None):
+        if 0 in halves and picked is not behind:
 
             @only(has_t(me), ot == n)
             def _():
                 own_t(t).start()
 
         if len(halves) == 2:
-            started(functools.partial(t1, t), has_t, ot)
+            started(functools.partial(t1, t), has_t, ot, pick=picked)
         else:
             started(functools.partial(t1, t), has_t, ot, 2 - halves[0], 2)
 
@@ -443,6 +453,21 @@
     def gram_done(k):
         ref = grams[k][2]
         counted(has_g(k), g_count(k), lambda m: whole(ref.at[pl.ds(0, m)], g_send.at[k, 1], g_recv.at[k, 1]), take)
+
+    def gram_clear(k):
+        land = grams[k][1]
+        counted(has_g(k), g_count(k), lambda m: whole(land.at[pl.ds(0, m)], g_send.at[k, 0], g_recv.at[k, 0]), clear)
+        once(has_g(k), g_count(k), lambda m: whole(land.at[pl.ds(0, m)], g_send.at[k, 1], g_recv.at[k, 1]), clear)
+
+    def far_copy(to):
+        return pltpu.make_async_remote_copy(
+            src_ref=far_sum,
+            dst_ref=far_sum,
+            send_sem=h_send.at[0],
+            recv_sem=h_recv.at[0],
+            device_id={"cols": to},
+            device_id_type=MESH,
+        )
 
     def has_c(j):
         return j < oc
@@ -609,14 +634,7 @@
 
     started(p1, has_p, op)
 
-    def ahead(d):
-        return (d == 2) | (d == 4)
-
-    @only(has_t(me), ot == n)
-    def _():
-        own_t(0).start()
-
-    started(functools.partial(t1, 0), has_t, ot, pick=ahead)
+    start_t1(0, picked=ahead)
 
     @only(has_p(me), op == n)
     def _():
@@ -654,7 +672,7 @@
             compose(ring_p.at[t], shifts[t], me, keep)
 
     last = tt - 1
-    started(functools.partial(t1, 0), has_t, ot, pick=lambda d: jnp.logical_not(ahead(d)))
+    start_t1(0, picked=behind)
     if tt > 1:
         start_t1(1)
     counted(has_p, op, lambda k: whole(full.at[z, pl.ds(0, k * tp)], p2_send.at[0], p2_recv.at[0]), take)
@@ -747,18 +765,12 @@
             send_factor(i, 0, start_copy)
             if i == 0:
                 forward(middle, range(pieces - 1, pieces))
-                gram_far()
-                gram_scatter(1)
-                if last > 1:
-                    start_t1(last, (0,))
+                rest_t1()
                 for t in range(2, last):
                     turn_t(t)
             if i == min(1, tiles - 2):
-                gram_spread(1)
-                if last > 1:
-                    start_t1(last, (1,))
                 rest_t2()
-        gram_done(1)
+        far_copy(helper_z).wait_recv()
         border()
         factor_tile(tiles - 1)
         send_factor(tiles - 1, 0, start_copy)
@@ -767,11 +779,7 @@
         finish_turns()
         for t in range(early):
             cross_chunk(t)
-        for k in (0, 1):
-            part, land, _ = grams[k]
-            row = lambda m: pl.ds(0, m)
-            counted(has_g(k), g_count(k), lambda m: whole(land.at[row(m)], g_send.at[k, 0], g_recv.at[k, 0]), clear)
-            once(has_g(k), g_count(k), lambda m: whole(land.at[row(m)], g_send.at[k, 1], g_recv.at[k, 1]), clear)
+        gram_clear(0)
 
     @pl.when(follows)
     def _():
@@ -784,8 +792,29 @@
         if last < 2:
             for d in range(middle, middle + 1):
                 forward(d)
-        rest_t1()
+
+        @pl.when(helps)
+        def _():
+            gram_far()
+            gram_scatter(1)
+            if last > 1:
+                start_t1(last, picked=ahead)
+            gram_spread(1)
+            if last > 1:
+                start_t1(last, picked=behind)
+
+        @pl.when(jnp.logical_not(helps))
+        def _():
+            rest_t1()
+
         rest_t2()
+
+        @pl.when(helps)
+        def _():
+            gram_done(1)
+            far_copy(lead_z).start()
+            gram_clear(1)
+
         finish_turns()
         for d in range(middle + 1, depth):
             forward(d)
@@ -794,19 +823,22 @@
         factor_whole(0).wait_recv()
 
     make_basis()
-    for t in range(early, last):
+    for t in range(early, tt):
         cross_chunk(t)
-    cross_chunk(last)
-    for t in range(last):
+    for t in range(tt):
         cross_spread(t)
-    cross_spread(last)
-    if last > 0:
-        emit(list(range(last)))
-    cross_done(last)
+    if early > 0:
+        emit(list(range(early)))
+    for t in range(early, tt):
+        cross_done(t)
 
     @pl.when(follows)
     def _():
         factor_whole(1).wait_recv()
+
+    @pl.when(helps)
+    def _():
+        far_copy(lead_z).wait_send()
 
     @pl.when(leads)
     def _():
@@ -903,6 +935,8 @@
             dma((2, tt)),
             dma((depth, 2)),
             dma((2,)),
+            dma((1,)),
+            dma((1,)),
             dma((1 + tt,)),
         ]
         + [pltpu.VMEM((total + blocks, SUB, BW), F32)] * tt,
@@ -982,7 +1016,7 @@
 def final(upper, inv, cross, q, reg, high, low, root):
     size = inv.shape[0]
     ot, tt = reg.shape[:2]
-    early = tt - 1
+    early = min(2, tt - 1)
     vmem = pl.BlockSpec(memory_space=pltpu.VMEM)
     hbm = pl.BlockSpec(memory_space=pl.ANY)
     near = [pltpu.with_memory_space_constraint(x, pltpu.VMEM) for x in (upper, inv, cross, q, reg, high, low)]

time: 139 us -> 136 us (0.978)
  Pallas kernels: 138 us -> 135 us
    pallas_call x1, Pallas kernels: 135 us -> 132 us  [fused(): pl.pallas_call(functools.partial(fused_kernel, n, depth, pieces, root), o...]
where the time goes in v5:
time: 136 us
  Pallas kernels  135 us (99%)
    pallas_call x1, Pallas kernels, fused(): pl.pallas_call(functools.partial(fused_kernel, n, depth, pieces, root), o...  132 us
    pallas_call x1, Pallas kernels, final(): pl.pallas_call(functools.partial(final_kernel, root, early), out_shape=(j...  3.17 us

profile of v5, /device:TPU:9, one launch (start us, length us, event | category | flops | bytes accessed | tf_op | source)
XLA Modules:
  0.0 136.3 jit_solution(29507075555993769)
XLA Ops:
  0.6 132.3 %shard_map.75 = (f32[256,256]{1,0:T(8,128)S(1)}, f32[256,256]{1,0:T(8,128)S(1)}, f32[4,8,8,256]{3,2,1,0:T(8,128)S(1)}, f32[8,32,8,128]{3,2,1,0:T(8,128)S(1)}, f3...) custom-call(s32[64]{0:T(128)} %panel_shift.1, ...), custom_call_target="tpu_custom_call" | custom-call | bytes 167772160 | tf_op jit(solution)/shard_map/pallas_call | solution.py:893
  132.9 3.2 %shard_map.76 = (f32[256,256]{1,0:T(8,128)}, f32[256,256]{1,0:T(8,128)}, f32[8,32,8,128]{3,2,1,0:T(8,128)}, f32[8,4,32,8,128]{4,3,2,1,0:T(8,128)}) custom-call(f32[256,256]{1,0:T(8,128)S(1)} %get-tuple-element.15.upper, f32[256,256]{1,0:T(8,128)S(1)} %get-tuple-element.16.inv, f32[4,8,8,256]{3,2,1,0:T(8,128)S(1)} %get-tuple-element.17.cross, ...), custom_call_target="tpu_custom_call" | custom-call | flops 536870912 | bytes 8388608 | tf_op jit(solution)/shard_map/pallas_call | solution.py:1023

commit v6 on v5

--- a/solution.py
+++ b/solution.py
@@ -324,7 +324,7 @@
                         line(side, d + 1, q).start()
 
     def ahead(d):
-        return (d == 2) | (d == 4)
+        return (d == 2) | (d == 4) | (d == 6)
 
     def behind(d):
         return jnp.logical_not(ahead(d))
@@ -882,7 +882,7 @@
     edge = size - tile
     packed = tile * (tiles * (tiles - 1) // 2)
     far_rows = -(-tile // (n * SUB)) * SUB
-    pieces = 4 if ctp % 4 == 0 else 1
+    pieces = 2 if ctp % 2 == 0 else 1
     total = n * blocks
     smem = pl.BlockSpec(memory_space=pltpu.SMEM)
     vmem = pl.BlockSpec(memory_space=pltpu.VMEM)

time: 136 us -> 135 us (level)
  Pallas kernels: 135 us -> 133 us
    pallas_call x1, Pallas kernels: 132 us -> 130 us  [fused(): pl.pallas_call(functools.partial(fused_kernel, n, depth, pieces, root), o...]
where the time goes in v6:
time: 135 us; the launch traced here: 134 us
  Pallas kernels  133 us (99%)
    pallas_call x1, Pallas kernels, fused(): pl.pallas_call(functools.partial(fused_kernel, n, depth, pieces, root), o...  130 us
    pallas_call x1, Pallas kernels, final(): pl.pallas_call(functools.partial(final_kernel, root, early), out_shape=(j...  3.17 us

profile of v6, /device:TPU:9, one launch (start us, length us, event | category | flops | bytes accessed | tf_op | source)
XLA Modules:
  0.0 134.0 jit_solution(13822941161134784030)
XLA Ops:
  0.6 130.0 %shard_map.75 = (f32[256,256]{1,0:T(8,128)S(1)}, f32[256,256]{1,0:T(8,128)S(1)}, f32[4,8,8,256]{3,2,1,0:T(8,128)S(1)}, f32[8,32,8,128]{3,2,1,0:T(8,128)S(1)}, f3...) custom-call(s32[64]{0:T(128)} %panel_shift.1, ...), custom_call_target="tpu_custom_call" | custom-call | bytes 167772160 | tf_op jit(solution)/shard_map/pallas_call | solution.py:893
  130.6 3.2 %shard_map.76 = (f32[256,256]{1,0:T(8,128)}, f32[256,256]{1,0:T(8,128)}, f32[8,32,8,128]{3,2,1,0:T(8,128)}, f32[8,4,32,8,128]{4,3,2,1,0:T(8,128)}) custom-call(f32[256,256]{1,0:T(8,128)S(1)} %get-tuple-element.15.upper, f32[256,256]{1,0:T(8,128)S(1)} %get-tuple-element.16.inv, f32[4,8,8,256]{3,2,1,0:T(8,128)S(1)} %get-tuple-element.17.cross, ...), custom_call_target="tpu_custom_call" | custom-call | flops 536870912 | bytes 8388608 | tf_op jit(solution)/shard_map/pallas_call | solution.py:1023

commit v7 on v6

--- a/solution.py
+++ b/solution.py
@@ -971,7 +971,7 @@
     ot, tt, blocks = reg.shape[:3]
     rows_t = ot * SUB
     chunks = list(range(early, tt))
-    steps = 2 if blocks % 2 == 0 else 1
+    steps = 4 if blocks % 4 == 0 else 1
     span = blocks // steps
     copies = [pltpu.make_async_copy(q, q_ref, sems.at[0])]
     copies.append(pltpu.make_async_copy(upper, r_ref, sems.at[1]))
@@ -1033,7 +1033,7 @@
         scratch_shapes=[
             pltpu.VMEM((ot, tt - early) + reg.shape[2:], F32),
             pltpu.VMEM((size, ot * tt * SUB), F32),
-            pltpu.SemaphoreType.DMA((3 + early + 2 * (tt - early),)),
+            pltpu.SemaphoreType.DMA((3 + early + 4 * (tt - early),)),
         ],
         compiler_params=pltpu.CompilerParams(vmem_limit_bytes=24 << 20),
         cost_estimate=pl.CostEstimate(

time: 135 us -> 134 us (level)
  no operation moved by 1% of the time
where the time goes in v7:
time: 134 us; the launch traced here: 133 us
  Pallas kernels  133 us (99%)
    pallas_call x1, Pallas kernels, fused(): pl.pallas_call(functools.partial(fused_kernel, n, depth, pieces, root), o...  130 us
    pallas_call x1, Pallas kernels, final(): pl.pallas_call(functools.partial(final_kernel, root, early), out_shape=(j...  2.69 us

profile of v7, /device:TPU:9, one launch (start us, length us, event | category | flops | bytes accessed | tf_op | source)
XLA Modules:
  0.0 133.5 jit_solution(419851027448412006)
XLA Ops:
  0.6 130.0 %shard_map.75 = (f32[256,256]{1,0:T(8,128)S(1)}, f32[256,256]{1,0:T(8,128)S(1)}, f32[4,8,8,256]{3,2,1,0:T(8,128)S(1)}, f32[8,32,8,128]{3,2,1,0:T(8,128)S(1)}, f3...) custom-call(s32[64]{0:T(128)} %panel_shift.1, ...), custom_call_target="tpu_custom_call" | custom-call | bytes 167772160 | tf_op jit(solution)/shard_map/pallas_call | solution.py:893
  130.6 2.7 %shard_map.76 = (f32[256,256]{1,0:T(8,128)}, f32[256,256]{1,0:T(8,128)}, f32[8,32,8,128]{3,2,1,0:T(8,128)}, f32[8,4,32,8,128]{4,3,2,1,0:T(8,128)}) custom-call(f32[256,256]{1,0:T(8,128)S(1)} %get-tuple-element.15.upper, f32[256,256]{1,0:T(8,128)S(1)} %get-tuple-element.16.inv, f32[4,8,8,256]{3,2,1,0:T(8,128)S(1)} %get-tuple-element.17.cross, ...), custom_call_target="tpu_custom_call" | custom-call | flops 536870912 | bytes 8388608 | tf_op jit(solution)/shard_map/pallas_call | solution.py:1023
